TPU v7x, 128 devices: a whole 4x4x4 slice. The times are simulated.
128 devices in a mesh: src: 32 (over x, z, core), tgt: 4 (over y).
Axes of the slice: x: 4, y: 4, z: 4, core: 2. Of those that a mesh axis runs over, the one named last changes fastest.
Arguments:
- features: bfloat16 [65536, 1024], P('src', 'tgt'), may hold values from -6 to 6
- cites_tiles: bfloat16 [6144, 128, 128], P('src'), may hold values from -0.0546875 to 0.0546875
- cites_targets: int32 [6144], P('src'), may hold values from 0 to 31
- cites_sources: int32 [6144], P('src'), may hold values from 0 to 15
- cites_counts: int32 [32], P('src'), may hold values from 1 to 192, 3072 in all
- writes_tiles: bfloat16 [3072, 128, 128], P('src'), may hold values from -0.078125 to 0.078125
- writes_targets: int32 [3072], P('src'), may hold values from 0 to 31
- writes_sources: int32 [3072], P('src'), may hold values from 0 to 15
- writes_counts: int32 [32], P('src'), may hold values from 1 to 96, 1536 in all
- topic_tiles: bfloat16 [1536, 128, 128], P('src'), may hold values from -0.109375 to 0.109375
- topic_targets: int32 [1536], P('src'), may hold values from 0 to 31
- topic_sources: int32 [1536], P('src'), may hold values from 0 to 15
- topic_counts: int32 [32], P('src'), may hold values from 1 to 48, 768 in all
- owner_map: int32 [32], replicated, may hold values from 0 to 31, each once
- weights: bfloat16 [3, 1024, 1024], P(None, 'tgt'), may hold values from -0.1875 to 0.1875
- bias_row: bfloat16 [1024], P('tgt'), may hold values from -3 to 3
- cotangent: bfloat16 [4096, 1024], P('src', 'tgt'), may hold values from -6 to 6
Outputs:
- mixed_out: bfloat16 [4096, 1024], P('src', 'tgt')
- grad_weight: float32 [3, 1024, 1024], P(None, 'tgt', 'src')
- grad_source: bfloat16 [65536, 1024], P('src', 'tgt')
Inputs may be any that keep to these rules, and one draw needn't show every extreme that they name: `cites_targets`: target block of a slot; only live slots are read. `cites_sources`: source block within the slot's own partition. `cites_counts`: live slots come first in each partition's 192 slots; they sum to 3072. `writes_targets`: target block of a slot; only live slots are read. `writes_sources`: source block within the slot's own partition. `writes_counts`: live slots come first in each partition's 96 slots; they sum to 1536. `topic_targets`: target block of a slot; only live slots are read. `topic_sources`: source block within the slot's own partition. `topic_counts`: live slots come first in each partition's 48 slots; they sum to 768. `owner_map`: A permutation of the target blocks.
All inputs are finite; a program needn't handle non-finite values.
Results may differ from a plain program's by a relative error of at most 0.015.
Values may be sent and summed in bfloat16 or wider, within the bound.
No kernel may reach another device: no remote copies, remote signals or barrier semaphores. Data moves between devices by JAX's collectives and lax.ppermute only.
A program may use at most 128 MiB of HBM per device.

v0:
```python
import jax
import jax.numpy as jnp
from jax import lax
from jax.sharding import PartitionSpec as P

TILE = 128


def gelu_tanh(values):
    return jax.nn.gelu(values, approximate=True)


def slot_numbers(tile_targets, owner_map):
    columns = jnp.arange(owner_map.shape[0], dtype=jnp.int32)
    return jnp.sum(
        jnp.where(tile_targets[:, None] == owner_map[None, :], columns[None, :], 0), axis=1
    )


def gather_sums(tile_values, slot_list, tile_sources, tile_count, source_blocks, blocks):
    capacity = tile_values.shape[0]
    stride = min(48, capacity)
    feature_width = source_blocks.shape[2]
    living = (jnp.arange(capacity, dtype=jnp.int32) < tile_count[0]).astype(jnp.float32)

    def gather_one_block(totals, position):
        offset = position * stride
        values_part = lax.dynamic_slice_in_dim(tile_values, offset, stride, 0)
        sources_part = lax.dynamic_slice_in_dim(tile_sources, offset, stride, 0)
        slots_part = lax.dynamic_slice_in_dim(slot_list, offset, stride, 0)
        living_part = lax.dynamic_slice_in_dim(living, offset, stride, 0)
        picked = jnp.take(source_blocks, sources_part, axis=0)
        product = jnp.einsum(
            "ctk,ckd->ctd", values_part, picked, preferred_element_type=jnp.float32
        )
        product = product * living_part[:, None, None]
        totals = totals + jax.ops.segment_sum(product, slots_part, num_segments=blocks)
        return (totals, None)

    start_sums = jnp.zeros((blocks, TILE, feature_width), jnp.float32)
    totals = lax.scan(
        gather_one_block, start_sums, jnp.arange(capacity // stride, dtype=jnp.int32)
    )[0]
    return totals.reshape(blocks, TILE * feature_width)


def spread_sums(tile_values, slot_list, tile_sources, tile_count, messages, source_count):
    capacity = tile_values.shape[0]
    stride = min(48, capacity)
    feature_width = messages.shape[2]
    living = (jnp.arange(capacity, dtype=jnp.int32) < tile_count[0]).astype(jnp.float32)

    def spread_one_block(totals, position):
        offset = position * stride
        values_part = lax.dynamic_slice_in_dim(tile_values, offset, stride, 0)
        sources_part = lax.dynamic_slice_in_dim(tile_sources, offset, stride, 0)
        slots_part = lax.dynamic_slice_in_dim(slot_list, offset, stride, 0)
        living_part = lax.dynamic_slice_in_dim(living, offset, stride, 0)
        picked = jnp.take(messages, slots_part, axis=0)
        product = jnp.einsum(
            "ctk,ctd->ckd", values_part, picked, preferred_element_type=jnp.float32
        )
        product = product * living_part[:, None, None]
        totals = totals + jax.ops.segment_sum(product, sources_part, num_segments=source_count)
        return (totals, None)

    start_sums = jnp.zeros((source_count, TILE, feature_width), jnp.float32)
    return lax.scan(spread_one_block, start_sums, jnp.arange(capacity // stride, dtype=jnp.int32))[
        0
    ]


def shards(
    features,
    cites_tiles,
    cites_targets,
    cites_sources,
    cites_counts,
    writes_tiles,
    writes_targets,
    writes_sources,
    writes_counts,
    topic_tiles,
    topic_targets,
    topic_sources,
    topic_counts,
    owner_map,
    weights,
    bias_row,
    cotangent,
):
    blocks = lax.axis_size("src")
    feature_width = features.shape[1]
    source_blocks = features.reshape(-1, TILE, feature_width)
    source_count = source_blocks.shape[0]
    relations = (
        (cites_tiles, cites_targets, cites_sources, cites_counts),
        (writes_tiles, writes_targets, writes_sources, writes_counts),
        (topic_tiles, topic_targets, topic_sources, topic_counts),
    )
    slot_lists = [slot_numbers(relation[1], owner_map) for relation in relations]
    partials = [
        gather_sums(relation[0], slot_list, relation[2], relation[3], source_blocks, blocks)
        for relation, slot_list in zip(relations, slot_lists)
    ]
    reduced = (
        lax.psum_scatter(partials[0], "src", scatter_dimension=0, tiled=True),
        lax.psum_scatter(partials[1], "src", scatter_dimension=0, tiled=True),
        lax.psum_scatter(partials[2], "src", scatter_dimension=0, tiled=True),
    )
    rounded = [part_sum.reshape(TILE, feature_width).astype(jnp.bfloat16) for part_sum in reduced]
    hidden_terms = jnp.dot(rounded[0], weights[0], preferred_element_type=jnp.float32)
    for number in range(1, 3):
        hidden_terms = hidden_terms + jnp.dot(
            rounded[number], weights[number], preferred_element_type=jnp.float32
        )
    hidden = (
        lax.psum_scatter(hidden_terms, "tgt", scatter_dimension=1, tiled=True)
        + bias_row.astype(jnp.float32)[None, :]
    )
    mixed_out, pullback = jax.vjp(gelu_tanh, hidden)
    grad_hidden = pullback(cotangent.astype(jnp.float32))[0].astype(jnp.bfloat16)
    full_grad = lax.all_gather(grad_hidden, "tgt", axis=1, tiled=True)
    weight_terms = jnp.stack(
        [
            lax.dot_general(
                rounded[number],
                full_grad,
                (((0,), (0,)), ((), ())),
                preferred_element_type=jnp.float32,
            )
            for number in range(3)
        ]
    )
    grad_weight = lax.psum_scatter(
        weight_terms.astype(jnp.bfloat16), "src", scatter_dimension=2, tiled=True
    ).astype(jnp.float32)

    def form_messages(row_piece):
        return jnp.stack(
            [
                lax.dot_general(
                    row_piece,
                    weights[number],
                    (((1,), (1,)), ((), ())),
                    preferred_element_type=jnp.float32,
                )
                for number in range(3)
            ]
        ).astype(jnp.bfloat16)

    messages = form_messages(lax.all_gather(full_grad, "src", axis=0, tiled=True))
    messages = messages.reshape(3, blocks, TILE, feature_width)
    grad_total = spread_sums(
        relations[0][0], slot_lists[0], relations[0][2], relations[0][3], messages[0], source_count
    )
    for number in range(1, 3):
        grad_total = grad_total + spread_sums(
            relations[number][0],
            slot_lists[number],
            relations[number][2],
            relations[number][3],
            messages[number],
            source_count,
        )
    grad_source = grad_total.reshape(source_count * TILE, feature_width).astype(jnp.bfloat16)
    return (mixed_out.astype(jnp.bfloat16), grad_weight, grad_source)


def solution(mesh):
    in_specs = (
        P("src", "tgt"),
        P("src", None, None),
        P("src"),
        P("src"),
        P("src"),
        P("src", None, None),
        P("src"),
        P("src"),
        P("src"),
        P("src", None, None),
        P("src"),
        P("src"),
        P("src"),
        P(),
        P(None, "tgt", None),
        P("tgt"),
        P("src", "tgt"),
    )
    out_specs = (P("src", "tgt"), P(None, "tgt", "src"), P("src", "tgt"))
    return jax.shard_map(shards, mesh=mesh, in_specs=in_specs, out_specs=out_specs, check_vma=False)
```

profile of v0, /device:TPU:1, one launch (start us, length us, event | category | flops | bytes accessed | tf_op | source)
XLA Modules:
  0.0 838.1 jit_solution(3164162358513415100)
XLA Ops:
  13.1 6.0 multiply_bitcast_fusion.1
  19.1 6.6 copy.42
  28.4 14.6 %scatter_fusion.4 = f32[32,128,256]{2,1,0:T(8,128)} fusion(f32[32,128,256]{2,1,0:T(8,128)} %broadcast.48.clone.2, s32[48]{0:T(128)S(1)} %select_reduce_fusion.1, f32[48,128,256]{2,1,0:T(8,128)} %copy.42), kind=kCustom, calls=%fused_computation.10 | custom fusion | flops 1572864 | bytes 18874560 | tf_op jit(solution)/shard_map/while/body/eval_jaxpr/scatter-add | solution.py:37
  43.0 6.7 copy.55
  53.0 99.0 %while.48 = (s32[]{:T(128)}, f32[32,128,256]{2,1,0:T(8,128)}, s32[4]{0:T(128)S(1)}, s32[192]{0:T(256)S(1)}, bf16[192,128,128]{2,1,0:T(8,128)(2,1)}, /*index=5*/s...) while((s32[]{:T(128)}, f32[32,128,256]{2,1,0:T(8,128)}, ...), condition=%wide.region_3.5_spmd, body=%wide.region_1.0_spmd.sunk | while | flops 407373088 | bytes 36182176 | solution.py:41
  57.0 6.1 broadcast_multiply_fusion.8
  63.2 14.5 %scatter_fusion = f32[32,128,256]{2,1,0:T(8,128)} fusion(f32[32,128,256]{2,1,0:T(8,128)} %get-tuple-element.599, s32[48]{0:T(128)S(1)} %dynamic_slice.117, f32[48,128,256]{2,1,0:T(8,128)} %broadcast_multiply_fusion.8), kind=kCustom, calls=%fused_computation.6.clone.1 | custom fusion | flops 1572864 | bytes 18874560 | tf_op jit(solution)/shard_map/while/body/eval_jaxpr/scatter-add | solution.py:37
  81.6 6.1 broadcast_multiply_fusion.8
  87.8 14.6 %scatter_fusion = f32[32,128,256]{2,1,0:T(8,128)} fusion(f32[32,128,256]{2,1,0:T(8,128)} %get-tuple-element.599, s32[48]{0:T(128)S(1)} %dynamic_slice.117, f32[48,128,256]{2,1,0:T(8,128)} %broadcast_multiply_fusion.8), kind=kCustom, calls=%fused_computation.6.clone.1 | custom fusion | flops 1572864 | bytes 18874560 | tf_op jit(solution)/shard_map/while/body/eval_jaxpr/scatter-add | solution.py:37
  106.4 6.1 broadcast_multiply_fusion.8
  112.5 14.6 %scatter_fusion = f32[32,128,256]{2,1,0:T(8,128)} fusion(f32[32,128,256]{2,1,0:T(8,128)} %get-tuple-element.599, s32[48]{0:T(128)S(1)} %dynamic_slice.117, f32[48,128,256]{2,1,0:T(8,128)} %broadcast_multiply_fusion.8), kind=kCustom, calls=%fused_computation.6.clone.1 | custom fusion | flops 1572864 | bytes 18874560 | tf_op jit(solution)/shard_map/while/body/eval_jaxpr/scatter-add | solution.py:37
  131.2 6.1 broadcast_multiply_fusion.8
  137.3 14.7 %scatter_fusion = f32[32,128,256]{2,1,0:T(8,128)} fusion(f32[32,128,256]{2,1,0:T(8,128)} %get-tuple-element.599, s32[48]{0:T(128)S(1)} %dynamic_slice.117, f32[48,128,256]{2,1,0:T(8,128)} %broadcast_multiply_fusion.8), kind=kCustom, calls=%fused_computation.6.clone.1 | custom fusion | flops 1572864 | bytes 18874560 | tf_op jit(solution)/shard_map/while/body/eval_jaxpr/scatter-add | solution.py:37
  152.0 6.7 copy.53
  161.9 49.9 %while.49 = (s32[]{:T(128)}, f32[32,128,256]{2,1,0:T(8,128)}, s32[2]{0:T(128)S(1)}, s32[96]{0:T(128)S(1)}, bf16[96,128,128]{2,1,0:T(8,128)(2,1)}, /*index=5*/s32...) while((s32[]{:T(128)}, f32[32,128,256]{2,1,0:T(8,128)}, ...), condition=%wide.region_8.10_spmd, body=%wide.region_6.9_spmd.sunk | while | flops 407373088 | bytes 36182176 | solution.py:41
  166.3 6.1 broadcast_multiply_fusion.9
  172.5 14.6 %scatter_fusion.1 = f32[32,128,256]{2,1,0:T(8,128)} fusion(f32[32,128,256]{2,1,0:T(8,128)} %get-tuple-element.635, s32[48]{0:T(128)S(1)} %dynamic_slice.121, f32[48,128,256]{2,1,0:T(8,128)} %broadcast_multiply_fusion.9), kind=kCustom, calls=%fused_computation.8.clone.1 | custom fusion | flops 1572864 | bytes 18874560 | tf_op jit(solution)/shard_map/while/body/eval_jaxpr/scatter-add | solution.py:37
  191.0 6.1 broadcast_multiply_fusion.9
  197.2 14.6 %scatter_fusion.1 = f32[32,128,256]{2,1,0:T(8,128)} fusion(f32[32,128,256]{2,1,0:T(8,128)} %get-tuple-element.635, s32[48]{0:T(128)S(1)} %dynamic_slice.121, f32[48,128,256]{2,1,0:T(8,128)} %broadcast_multiply_fusion.9), kind=kCustom, calls=%fused_computation.8.clone.1 | custom fusion | flops 1572864 | bytes 18874560 | tf_op jit(solution)/shard_map/while/body/eval_jaxpr/scatter-add | solution.py:37
  211.8 6.6 copy.54
  219.0 179.9 %all-reduce.9 = (bf16[32,32768]{1,0:T(8,128)(2,1)}, bf16[32,32768]{1,0:T(8,128)(2,1)}, bf16[32,32768]{1,0:T(8,128)(2,1)}) all-reduce(f32[32,32768]{1,0:T(8,128)} %bitcast.77, f32[32,32768]{1,0:T(8,128)} %bitcast.78, f32[32,32768]{1,0:T(8,128)} %bitcast.76), channel_id=2, replica_groups=mesh['src'=32,'tgt'=4] {'src'}, use_global_device_ids=true, to_apply=%region_4.6.clone | all-reduce | flops 3145728 | bytes 18874368
  406.9 20.9 %reduce-scatter.2.cloned.1.call-done = f32[128,256]{1,0:T(8,128)} async-done(((f32[128,1024]{1,0:T(8,128)}), f32[128,256]{1,0:T(8,128)}) %reduce-scatter.2.cloned.1.call-update) | async-done | bytes 131088 | tf_op jit(solution)/shard_map/reduce_scatter | solution.py:118
  429.5 9.9 %all_gather.6 = bf16[128,1024]{1,0:T(8,128)(2,1)S(1)} all-gather(bf16[128,256]{1,0:T(8,128)(2,1)S(1)} %get-tuple-element.370), channel_id=1, replica_groups=mesh['src'=32,'tgt'=4] {'tgt'}, dimensions={1}, use_global_device_ids=true | all-gather | bytes 327680 | tf_op jit(solution)/shard_map/all_gather | solution.py:123
  444.6 110.9 %all-reduce.8.cloned.1.call-done = bf16[3,256,1024]{1,0,2:T(4,128)(2,1)} async-done(((bf16[3,256,1024]{1,0,2:T(4,128)(2,1)}), bf16[3,256,1024]{1,0,2:T(4,128)(2,1)}) %all-reduce.8.cloned.1.call-update) | async-done | bytes 1572880
  557.0 54.2 %all-gather.2.cloned.1.call-done = bf16[4096,1024]{1,0:T(8,128)(2,1)} async-done(((bf16[128,1024]{1,0:T(8,128)(2,1)}), bf16[4096,1024]{1,0:T(8,128)(2,1)}) %all-gather.2.cloned.1.call-update) | async-done | bytes 8388624 | tf_op jit(solution)/shard_map/all_gather | solution.py:152
  611.2 7.2 convolution_convert_fusion.2
  620.0 105.0 %while.50 = (s32[]{:T(128)}, f32[16,128,256]{2,1,0:T(8,128)}, s32[4]{0:T(128)S(1)}, s32[192]{0:T(256)S(1)}, bf16[192,128,128]{2,1,0:T(8,128)(2,1)}, /*index=5*/s...) while((s32[]{:T(128)}, f32[16,128,256]{2,1,0:T(8,128)}, ...), condition=%wide.region_17.20_spmd, body=%wide.region_15.19_spmd.sunk | while | flops 407373088 | bytes 36182176 | solution.py:68
  621.3 4.1 gather_fusion.2
  625.5 6.4 broadcast_multiply_fusion.10
  631.9 14.2 %scatter_fusion.2 = f32[16,128,256]{2,1,0:T(8,128)} fusion(f32[16,128,256]{2,1,0:T(8,128)} %get-tuple-element.671, s32[48]{0:T(128)S(1)} %dynamic_slice.125, f32[48,128,256]{2,1,0:T(8,128)} %broadcast_multiply_fusion.10), kind=kCustom, calls=%fused_computation.7.clone.1 | custom fusion | flops 1572864 | bytes 18874560 | tf_op jit(solution)/shard_map/while/body/eval_jaxpr/scatter-add | solution.py:64
  651.6 6.4 broadcast_multiply_fusion.10
  658.0 14.4 %scatter_fusion.2 = f32[16,128,256]{2,1,0:T(8,128)} fusion(f32[16,128,256]{2,1,0:T(8,128)} %get-tuple-element.671, s32[48]{0:T(128)S(1)} %dynamic_slice.125, f32[48,128,256]{2,1,0:T(8,128)} %broadcast_multiply_fusion.10), kind=kCustom, calls=%fused_computation.7.clone.1 | custom fusion | flops 1572864 | bytes 18874560 | tf_op jit(solution)/shard_map/while/body/eval_jaxpr/scatter-add | solution.py:64
  677.9 6.4 broadcast_multiply_fusion.10
  684.4 14.3 %scatter_fusion.2 = f32[16,128,256]{2,1,0:T(8,128)} fusion(f32[16,128,256]{2,1,0:T(8,128)} %get-tuple-element.671, s32[48]{0:T(128)S(1)} %dynamic_slice.125, f32[48,128,256]{2,1,0:T(8,128)} %broadcast_multiply_fusion.10), kind=kCustom, calls=%fused_computation.7.clone.1 | custom fusion | flops 1572864 | bytes 18874560 | tf_op jit(solution)/shard_map/while/body/eval_jaxpr/scatter-add | solution.py:64
  704.1 6.4 broadcast_multiply_fusion.10
  710.6 14.4 %scatter_fusion.2 = f32[16,128,256]{2,1,0:T(8,128)} fusion(f32[16,128,256]{2,1,0:T(8,128)} %get-tuple-element.671, s32[48]{0:T(128)S(1)} %dynamic_slice.125, f32[48,128,256]{2,1,0:T(8,128)} %broadcast_multiply_fusion.10), kind=kCustom, calls=%fused_computation.7.clone.1 | custom fusion | flops 1572864 | bytes 18874560 | tf_op jit(solution)/shard_map/while/body/eval_jaxpr/scatter-add | solution.py:64
  725.0 7.1 convolution_convert_fusion.1
  733.7 52.7 %while.51 = (s32[]{:T(128)}, f32[16,128,256]{2,1,0:T(8,128)}, s32[2]{0:T(128)S(1)}, s32[96]{0:T(128)S(1)}, bf16[96,128,128]{2,1,0:T(8,128)(2,1)}, /*index=5*/s32...) while((s32[]{:T(128)}, f32[16,128,256]{2,1,0:T(8,128)}, ...), condition=%wide.region_20.23_spmd, body=%wide.region_18.22_spmd.sunk | while | flops 407373088 | bytes 36182176 | solution.py:68
  739.2 6.4 broadcast_multiply_fusion.11
  745.6 14.3 %scatter_fusion.3 = f32[16,128,256]{2,1,0:T(8,128)} fusion(f32[16,128,256]{2,1,0:T(8,128)} %get-tuple-element.707, s32[48]{0:T(128)S(1)} %dynamic_slice.129, f32[48,128,256]{2,1,0:T(8,128)} %broadcast_multiply_fusion.11), kind=kCustom, calls=%fused_computation.9.clone.1 | custom fusion | flops 1572864 | bytes 18874560 | tf_op jit(solution)/shard_map/while/body/eval_jaxpr/scatter-add | solution.py:64
  761.3 4.1 gather_fusion.3
  765.4 6.4 broadcast_multiply_fusion.11
  771.9 14.4 %scatter_fusion.3 = f32[16,128,256]{2,1,0:T(8,128)} fusion(f32[16,128,256]{2,1,0:T(8,128)} %get-tuple-element.707, s32[48]{0:T(128)S(1)} %dynamic_slice.129, f32[48,128,256]{2,1,0:T(8,128)} %broadcast_multiply_fusion.11), kind=kCustom, calls=%fused_computation.9.clone.1 | custom fusion | flops 1572864 | bytes 18874560 | tf_op jit(solution)/shard_map/while/body/eval_jaxpr/scatter-add | solution.py:64
  786.4 7.2 convolution_convert_fusion
  793.6 4.1 gather_fusion.5
  797.7 6.0 multiply_bitcast_fusion
  803.7 6.6 copy.47
  814.2 14.4 %scatter_fusion.5 = f32[16,128,256]{2,1,0:T(8,128)} fusion(f32[16,128,256]{2,1,0:T(8,128)} %add.128, s32[48]{0:T(128)S(1)} %copy-done.10, f32[48,128,256]{2,1,0:T(8,128)} %copy.47), kind=kCustom, calls=%fused_computation.11 | custom fusion | flops 1572864 | bytes 18874560 | tf_op jit(solution)/shard_map/while/body/eval_jaxpr/scatter-add | solution.py:64
  (152 shorter events, 80.6 us)
Async XLA Ops:
  7.2 5.9 copy-start
  7.2 420.6 %reduce-scatter.2.cloned.1.call-start = ((), (), s32[]{:S(2)}) async-start(), calls=%async_computation.1 | async-start | bytes 655360 | tf_op jit(solution)/shard_map/reduce_scatter | solution.py:118
  9.3 3.7 copy-start.8
  19.1 6.6 copy-start.12
  19.1 6.6 copy-start.13
  43.0 7.4 copy-start.11
  49.7 3.3 copy-start.1
  49.7 3.3 copy-start.7
  152.0 7.4 copy-start.14
  158.7 3.3 copy-start.6
  211.8 6.6 copy-start.16
  219.0 186.3 %copy-start.3 = (bf16[3,256,1024]{2,1,0:T(8,128)(2,1)S(1)}, bf16[3,256,1024]{2,1,0:T(8,128)(2,1)}, u32[]{:S(2)}) copy-start(bf16[3,256,1024]{2,1,0:T(8,128)(2,1)} %param.43) | copy-start | bytes 4718596
  398.9 8.0 copy-start.15
  398.9 28.9 %copy-start.5 = (bf16[128,256]{1,0:T(8,128)(2,1)S(1)}, bf16[128,256]{1,0:T(8,128)(2,1)}, u32[]{:S(2)}) copy-start(bf16[128,256]{1,0:T(8,128)(2,1)} %param.45) | copy-start | bytes 196612
  406.9 148.6 %all-reduce.8.cloned.1.call-start = ((), (), s32[]{:S(2)}) async-start(), calls=%async_computation.3 | async-start | bytes 4194304
  439.4 3.7 copy-start.2
  443.1 168.1 %all-gather.2.cloned.1.call-start = ((), (), s32[]{:S(2)}) async-start(), calls=%async_computation.2 | async-start | bytes 8650752 | tf_op jit(solution)/shard_map/all_gather | solution.py:152
  620.0 105.0 %copy-start.4 = (bf16[3,256,1024]{2,1,0:T(8,128)(2,1)S(1)}, bf16[3,256,1024]{2,1,0:T(8,128)(2,1)}, u32[]{:S(2)}) copy-start(bf16[3,256,1024]{2,1,0:T(8,128)(2,1)} %param.43) | copy-start | bytes 4718596
  793.6 4.1 copy-start.9
  810.3 3.9 copy-start.10
Sparse Core Ops, SparseCore 0:
  407.0 20.8 reduce-scatter.1
  443.3 112.1 all-reduce.7
  558.4 52.8 all-gather.1
where the time goes:
time: 849 us; the launch traced here: 838 us
  other arithmetic  215 us (25%)
  blocking collectives  190 us (22%)
  waiting for transfers between devices  187 us (22%)
  local copies, waits for them, and re-layouts  111 us (13%)
  matrix products  111 us (13%)
  between operations  16.9 us (2%)
  loops' own time  8.59 us (1%)
    unnamed x1, blocking collectives  180 us
    unnamed x4, waiting for transfers between devices  111 us
    scatter-add x7, other arithmetic, gather_one_block(): jax.ops.segment_sum(product, slots_part, num_segments=blocks)  102 us
    scatter-add x7, other arithmetic, spread_one_block(): jax.ops.segment_sum(product, sources_part, num_segments=source_count)  100 us
    all_gather x1, waiting for transfers between devices, shards(): lax.all_gather(full_grad, 'src', axis=0, tiled=True)  54.2 us
    dot_general x7, matrix products, spread_one_block(): jnp.einsum('ctk,ctd->ckd', values_part, picked, preferred_element_type=jn...  44.2 us
    dot_general x7, matrix products, gather_one_block(): jnp.einsum('ctk,ckd->ctd', values_part, picked, preferred_element_type=jn...  42.5 us
    gather x7, local copies, waits for them, and re-layouts, spread_one_block(): picked = jnp.take(messages, slots_part, axis=0)  28.5 us
  transfers between devices with their start and end apart: 3, of which 3 were waited for; matrix products, arithmetic and copies ran while one was open for 0% of the time, Pallas kernels for 0%

commit v1 on v0

v1 whole, which is shorter than its diff:
```python
import functools

import jax
import jax.numpy as jnp
from jax import lax
from jax.experimental import pallas as pl
from jax.experimental.pallas import tpu as pltpu
from jax.sharding import PartitionSpec as P

TILE = 128
SIDE = 4
GROUP = 8
BF16 = jnp.bfloat16
F32 = jnp.float32
VMEM_LIMIT = 60 * 1024 * 1024


def spec(space):
    return pl.BlockSpec(memory_space=space)


ANY, SMEM, VMEM = pl.ANY, pltpu.SMEM, pltpu.VMEM


def place_of(slot, place_ref):
    x, z, c = slot // 8, (slot // 2) % 4, slot % 2
    dx = (x - place_ref[0] + SIDE) % SIDE
    dz = (z - place_ref[1] + SIDE) % SIDE
    first = jnp.where(c == 0, dx, dz)
    second = jnp.where(c == 0, dz, dx)
    away = jnp.where(c == place_ref[2], 0, 16)
    return first, second, away


def start_tiles(tiles, counts, buffer, sems, bases):
    for number in range(3):
        def start(group, carry, number=number):
            offset = group * GROUP
            pltpu.make_async_copy(
                tiles[number].at[pl.ds(offset, GROUP)],
                buffer.at[pl.ds(bases[number] + offset, GROUP)],
                sems.at[bases[number] // GROUP + group],
            ).start()
            return carry

        lax.fori_loop(0, (counts[number][0] + GROUP - 1) // GROUP, start, 0)


def wait_tiles(tiles, buffer, sems, base, number, group):
    offset = group * GROUP
    pltpu.make_async_copy(
        tiles[number].at[pl.ds(offset, GROUP)],
        buffer.at[pl.ds(base + offset, GROUP)],
        sems.at[base // GROUP + group],
    ).wait()


def gather_kernel(
    place, owner_map,
    targets0, targets1, targets2, sources0, sources1, sources2, counts0, counts1, counts2,
    features, tiles0, tiles1, tiles2,
    keep, send,
    buffer, total, staged, table, tile_sems, out_sems,
):
    targets, sources = (targets0, targets1, targets2), (sources0, sources1, sources2)
    counts, tiles = (counts0, counts1, counts2), (tiles0, tiles1, tiles2)
    capacities = [t.shape[0] for t in tiles]
    bases = [0, capacities[0], capacities[0] + capacities[1]]
    start_tiles(tiles, counts, buffer, tile_sems, bases)

    def fill(slot, carry):
        first, second, away = place_of(slot, place)
        table[owner_map[slot]] = (away + first * SIDE + second) * 3
        return carry

    lax.fori_loop(0, 32, fill, 0)

    def clear(block, carry):
        total[block] = jnp.zeros(total.shape[1:], F32)
        return carry

    lax.fori_loop(0, 96, clear, 0)

    for number in range(3):
        def add_group(group, carry, number=number):
            wait_tiles(tiles, buffer, tile_sems, bases[number], number, group)
            products = []
            for lane in range(GROUP):
                j = group * GROUP + lane
                tile = buffer[bases[number] + j]
                block = features[sources[number][j]]
                products.append(jnp.dot(tile, block, preferred_element_type=F32))
            for lane in range(GROUP):
                j = group * GROUP + lane
                spot = jnp.where(j < counts[number][0], table[targets[number][j]] + number, 96)
                total[spot] += products[lane]
            return carry

        lax.fori_loop(0, (counts[number][0] + GROUP - 1) // GROUP, add_group, 0)

    def out_copy(where, spot):
        target = keep if where == 0 else send
        return pltpu.make_async_copy(
            staged.at[where * 16 + spot], target.at[spot], out_sems.at[where * 16 + spot]
        )

    for where in (1, 0):
        def emit(spot, carry, where=where):
            for number in range(3):
                staged[where * 16 + spot, pl.ds(number * TILE, TILE), :] = total[
                    (where * 16 + spot) * 3 + number
                ].astype(BF16)
            out_copy(where, spot).start()
            return carry

        lax.fori_loop(0, 16, emit, 0)
    for where in (1, 0):
        def finish(spot, carry, where=where):
            out_copy(where, spot).wait()
            return carry

        lax.fori_loop(0, 16, finish, 0)


def gather_sums(place, owner_map, relations, features):
    width = features.shape[-1]
    slots = sum(relation[0].shape[0] for relation in relations)
    blocks = jax.ShapeDtypeStruct((16, 3 * TILE, width), BF16)
    return pl.pallas_call(
        gather_kernel,
        out_shape=(blocks, blocks),
        in_specs=[spec(SMEM)] * 11 + [spec(VMEM)] + [spec(ANY)] * 3,
        out_specs=(spec(ANY), spec(ANY)),
        scratch_shapes=[
            pltpu.VMEM((slots, TILE, TILE), BF16),
            pltpu.VMEM((97, TILE, width), F32),
            pltpu.VMEM((32, 3 * TILE, width), BF16),
            pltpu.SMEM((32,), jnp.int32),
            pltpu.SemaphoreType.DMA((slots // GROUP,)),
            pltpu.SemaphoreType.DMA((32,)),
        ],
        compiler_params=pltpu.CompilerParams(vmem_limit_bytes=VMEM_LIMIT),
        name="gather_sums",
    )(
        place, owner_map,
        *[relation[1] for relation in relations],
        *[relation[2] for relation in relations],
        *[relation[3] for relation in relations],
        features.reshape(-1, TILE, width),
        *[relation[0] for relation in relations],
    )


def spread_kernel(
    place, owner_map,
    targets0, targets1, targets2, sources0, sources1, sources2, counts0, counts1, counts2,
    tiles0, tiles1, tiles2,
    own0, own3, own1, own2a, own2b, sib0, sib3, sib1, sib2a, sib2b,
    out,
    buffer, messages, total, table, tile_sems, in_sems,
):
    targets, sources = (targets0, targets1, targets2), (sources0, sources1, sources2)
    counts, tiles = (counts0, counts1, counts2), (tiles0, tiles1, tiles2)
    capacities = [t.shape[0] for t in tiles]
    bases = [0, capacities[0], capacities[0] + capacities[1]]
    pieces = [
        (own0, 0), (own3, 12), (own1, 4), (own2a, 8), (own2b, 10),
        (sib0, 16), (sib3, 28), (sib1, 20), (sib2a, 24), (sib2b, 26),
    ]
    copies = [
        pltpu.make_async_copy(
            piece, messages.at[pl.ds(at, piece.shape[0])], in_sems.at[number]
        )
        for number, (piece, at) in enumerate(pieces)
    ]
    for copy in copies:
        copy.start()
    start_tiles(tiles, counts, buffer, tile_sems, bases)

    def fill(slot, carry):
        first, second, away = place_of(slot, place)
        table[owner_map[slot]] = away + second * SIDE + first
        return carry

    lax.fori_loop(0, 32, fill, 0)

    def clear(block, carry):
        total[block] = jnp.zeros(total.shape[1:], F32)
        return carry

    lax.fori_loop(0, 16, clear, 0)
    for copy in copies:
        copy.wait()

    width = total.shape[1]
    for number in range(3):
        def add_group(group, carry, number=number):
            wait_tiles(tiles, buffer, tile_sems, bases[number], number, group)
            products = []
            for lane in range(GROUP):
                j = group * GROUP + lane
                tile = buffer[bases[number] + j]
                block = messages[table[targets[number][j]], pl.ds(number * width, width), :]
                products.append(jnp.dot(block, tile, preferred_element_type=F32))
            for lane in range(GROUP):
                j = group * GROUP + lane
                spot = jnp.where(j < counts[number][0], sources[number][j], 16)
                total[spot] += products[lane]
            return carry

        lax.fori_loop(0, (counts[number][0] + GROUP - 1) // GROUP, add_group, 0)

    def emit(block, carry):
        out[block] = total[block].T.astype(BF16)
        return carry

    lax.fori_loop(0, 16, emit, 0)


def spread_sums(place, owner_map, relations, pieces, width):
    slots = sum(relation[0].shape[0] for relation in relations)
    return pl.pallas_call(
        spread_kernel,
        out_shape=jax.ShapeDtypeStruct((16, TILE, width), BF16),
        in_specs=[spec(SMEM)] * 11 + [spec(ANY)] * 13,
        out_specs=spec(VMEM),
        scratch_shapes=[
            pltpu.VMEM((slots, TILE, TILE), BF16),
            pltpu.VMEM((32, 3 * width, TILE), BF16),
            pltpu.VMEM((17, width, TILE), F32),
            pltpu.SMEM((32,), jnp.int32),
            pltpu.SemaphoreType.DMA((slots // GROUP,)),
            pltpu.SemaphoreType.DMA((10,)),
        ],
        compiler_params=pltpu.CompilerParams(vmem_limit_bytes=VMEM_LIMIT),
        name="spread_sums",
    )(
        place, owner_map,
        *[relation[1] for relation in relations],
        *[relation[2] for relation in relations],
        *[relation[3] for relation in relations],
        *[relation[0] for relation in relations],
        *pieces,
    )


def columns_at(place, step, width):
    column = (place[3] + step) % SIDE
    return pl.ds(pl.multiple_of(column * width, width), width)


def hidden_kernel(place, part0, part1, part2, weights, rounded, terms0, terms1, terms2, terms3):
    width = part0.shape[1]
    whole = (part0[...].astype(F32) + part1[...].astype(F32) + part2[...].astype(F32)).astype(BF16)
    rounded[...] = whole
    for step, terms in enumerate((terms0, terms1, terms2, terms3)):
        value = jnp.zeros(terms.shape, F32)
        for number in range(3):
            value += jnp.dot(
                whole[number * TILE:(number + 1) * TILE],
                weights[number, :, columns_at(place, step, width)],
                preferred_element_type=F32,
            )
        terms[...] = value.astype(terms.dtype)


def hidden_terms(place, parts, weights):
    width = parts[0].shape[1]
    return pl.pallas_call(
        hidden_kernel,
        out_shape=(
            jax.ShapeDtypeStruct((3 * TILE, width), BF16),
            jax.ShapeDtypeStruct((TILE, width), F32),
            jax.ShapeDtypeStruct((TILE, width), BF16),
            jax.ShapeDtypeStruct((TILE, width), BF16),
            jax.ShapeDtypeStruct((TILE, width), BF16),
        ),
        in_specs=[spec(SMEM)] + [spec(VMEM)] * 4,
        out_specs=tuple([spec(VMEM)] * 5),
        name="hidden_terms",
    )(place, *parts, weights)


def message_kernel(place, grad0, grad1, grad2, grad3, weights, messages):
    width = grad0.shape[1]
    for number in range(3):
        value = jnp.zeros((width, TILE), F32)
        for step, grad in enumerate((grad0, grad1, grad2, grad3)):
            value += lax.dot_general(
                weights[number, :, columns_at(place, step, width)],
                grad[...],
                (((1,), (1,)), ((), ())),
                preferred_element_type=F32,
            )
        messages[pl.ds(number * width, width), :] = value.astype(BF16)


def form_messages(place, grads, weights):
    width = grads[0].shape[1]
    return pl.pallas_call(
        message_kernel,
        out_shape=jax.ShapeDtypeStruct((3 * width, TILE), BF16),
        in_specs=[spec(SMEM)] + [spec(VMEM)] * 5,
        out_specs=spec(VMEM),
        name="form_messages",
    )(place, *grads, weights)


def weight_kernel(place, grad0, grad1, grad2, grad3, rounded, keep, send):
    width = grad0.shape[1]
    for step, grad in enumerate((grad0, grad1, grad2, grad3)):
        block = (place[3] + step) % SIDE
        for number in range(3):
            value = lax.dot_general(
                grad[...],
                rounded[number * TILE:(number + 1) * TILE, :],
                (((0,), (0,)), ((), ())),
                preferred_element_type=F32,
            ).astype(BF16)
            columns = pl.ds(number * width, width)
            for part in range(8):
                first, second, away = place_of(block * 8 + part, place)
                spot = first * SIDE + second
                piece = value[part * 32:(part + 1) * 32]

                @pl.when(away == 0)
                def _():
                    keep[spot, :, columns] = piece

                @pl.when(away != 0)
                def _():
                    send[spot, :, columns] = piece


def weight_terms(place, grads, rounded):
    width = grads[0].shape[1]
    blocks = jax.ShapeDtypeStruct((16, 32, 3 * width), BF16)
    return pl.pallas_call(
        weight_kernel,
        out_shape=(blocks, blocks),
        in_specs=[spec(SMEM)] + [spec(VMEM)] * 5,
        out_specs=(spec(VMEM), spec(VMEM)),
        name="weight_terms",
    )(place, *grads, rounded)


def shift_pairs(step, second):
    pairs = []
    for s in range(32):
        x, z, c = s // 8, (s // 2) % 4, s % 2
        if (c == 0) != second:
            x = (x + step) % SIDE
        else:
            z = (z + step) % SIDE
        pairs.append((s, (x * SIDE + z) * 2 + c))
    return pairs


def shift(value, step, second=False):
    return lax.ppermute(value, "src", shift_pairs(step, second))


def swap(value):
    return lax.ppermute(value, "src", [(s, s ^ 1) for s in range(32)])


def add(*values):
    total = values[0].astype(F32)
    for value in values[1:]:
        total = total + value.astype(F32)
    return total.astype(BF16)


def ring_sum(keep, send):
    rows = keep.shape[1]
    got = swap(send)
    forth = shift(add(keep[8:10], got[8:10]), 1)
    back = shift(add(keep[10:12], got[10:12]), -1)
    one = jnp.concatenate([add(keep[4:6], got[4:6], forth), add(keep[6:8], got[6:8])])
    three = jnp.concatenate([add(keep[12:14], got[12:14]), add(keep[14:16], got[14:16], back)])
    forth, back = shift(one, 1), shift(three, -1)
    line = [add(keep[k], got[k], forth[k], back[k]) for k in range(4)]
    half = rows // 2
    forth = shift(line[2][:half], 1, True)
    back = shift(line[2][half:], -1, True)
    one = jnp.concatenate([add(line[1][:half], forth), line[1][half:]])
    three = jnp.concatenate([line[3][:half], add(line[3][half:], back)])
    return line[0], shift(one, 1, True), shift(three, -1, True)


def ring_gather(own):
    half = own.shape[0] // 2
    three, one = shift(own, 1), shift(own, -1)
    two = jnp.concatenate([shift(three[:half], 1), shift(one[half:], -1)])
    line = jnp.stack([own, one, two, three])
    three, one = shift(line, 1, True), shift(line, -1, True)
    return [line, three, one, shift(three[:2], 1, True), shift(one[2:], -1, True)]


def turn(value, step):
    return lax.ppermute(value, "tgt", [(t, (t + step) % SIDE) for t in range(SIDE)])


def shards(
    features,
    cites_tiles,
    cites_targets,
    cites_sources,
    cites_counts,
    writes_tiles,
    writes_targets,
    writes_sources,
    writes_counts,
    topic_tiles,
    topic_targets,
    topic_sources,
    topic_counts,
    owner_map,
    weights,
    bias_row,
    cotangent,
):
    width = features.shape[1]
    relations = (
        (cites_tiles, cites_targets, cites_sources, cites_counts),
        (writes_tiles, writes_targets, writes_sources, writes_counts),
        (topic_tiles, topic_targets, topic_sources, topic_counts),
    )
    s = lax.axis_index("src")
    place = jnp.stack([s // 8, (s // 2) % 4, s % 2, lax.axis_index("tgt")]).astype(jnp.int32)

    keep, send = gather_sums(place, owner_map, relations, features)
    parts = ring_sum(keep, send)

    rounded, terms0, terms1, terms2, terms3 = hidden_terms(place, parts, weights)
    hidden = (
        terms0
        + turn(terms1, 1).astype(F32)
        + turn(terms2, 2).astype(F32)
        + turn(terms3, 3).astype(F32)
        + bias_row.astype(F32)[None, :]
    )
    mixed_out, pullback = jax.vjp(functools.partial(jax.nn.gelu, approximate=True), hidden)
    grad_hidden = pullback(cotangent.astype(F32))[0].astype(BF16)
    grads = [grad_hidden, turn(grad_hidden, -1), turn(grad_hidden, -2), turn(grad_hidden, -3)]

    own = ring_gather(form_messages(place, grads, weights))
    sibling = [swap(piece) for piece in own]
    grad_source = spread_sums(place, owner_map, relations, own + sibling, width)

    weight_parts = ring_sum(*weight_terms(place, grads, rounded))
    weight_sum = sum(part.astype(F32) for part in weight_parts)
    grad_weight = weight_sum.reshape(32, 3, width).transpose(1, 2, 0)
    return (mixed_out.astype(BF16), grad_weight, grad_source.reshape(-1, width))


def solution(mesh):
    in_specs = (
        P("src", "tgt"),
        P("src", None, None),
        P("src"),
        P("src"),
        P("src"),
        P("src", None, None),
        P("src"),
        P("src"),
        P("src"),
        P("src", None, None),
        P("src"),
        P("src"),
        P("src"),
        P(),
        P(None, "tgt", None),
        P("tgt"),
        P("src", "tgt"),
    )
    out_specs = (P("src", "tgt"), P(None, "tgt", "src"), P("src", "tgt"))
    return jax.shard_map(shards, mesh=mesh, in_specs=in_specs, out_specs=out_specs, check_vma=False)
```

time: 849 us -> 176 us (0.21)
  other arithmetic: 215 us -> 14 us
  blocking collectives: 190 us -> 0 us
  waiting for transfers between devices: 187 us -> 58.6 us
  matrix products: 111 us -> 0 us
  local copies, waits for them, and re-layouts: 111 us -> 2.39 us
  starting transfers between devices: 0.29 us -> 58.2 us
  Pallas kernels: 0 us -> 36.8 us
  between operations: 16.9 us -> 3.11 us
  loops' own time: 8.59 us -> 0 us
    scatter-add x14 -> x0, other arithmetic: 203 us -> none  [the longest x7 102 us: gather_one_block(): jax.ops.segment_sum(product, slots_part, num_segments=blocks)]
    unnamed x1 -> x0, blocking collectives: 180 us -> none
    unnamed x4 -> x0, waiting for transfers between devices: 111 us -> none
    dot_general x23 -> x0, matrix products: 111 us -> none  [the longest x7 44.2 us: spread_one_block(): jnp.einsum('ctk,ctd->ckd', values_part, picked, preferred_element_type=jn...]
    ppermute x0 -> x37, waiting for transfers between devices: none -> 58.6 us  [the longest x24 43.5 us: shift(): return lax.ppermute(value, 'src', shift_pairs(step, second))]
    ppermute x0 -> x37, starting transfers between devices: none -> 58.2 us  [the longest x24 36.8 us: shift(): return lax.ppermute(value, 'src', shift_pairs(step, second))]
    all_gather x1 -> x0, waiting for transfers between devices: 54.2 us -> none  [shards(): lax.all_gather(full_grad, 'src', axis=0, tiled=True)]
    gather x14 -> x0, local copies, waits for them, and re-layouts: 47.8 us -> none  [the longest x7 28.5 us: spread_one_block(): picked = jnp.take(messages, slots_part, axis=0)]
  transfers between devices with their start and end apart: 3 -> 37, of which waited for: 3 -> 22; matrix products, arithmetic and copies ran while one was open for 0% -> 4% of each run, Pallas kernels for 0% -> 2%
where the time goes in v1:
time: 176 us; the launch traced here: 173 us
  waiting for transfers between devices  58.6 us (33%)
  starting transfers between devices  58.2 us (33%)
  Pallas kernels  36.8 us (21%)
  other arithmetic  14 us (8%)
  between operations  3.11 us (2%)
  local copies, waits for them, and re-layouts  2.39 us (1%)
    ppermute x24, waiting for transfers between devices, shift(): return lax.ppermute(value, 'src', shift_pairs(step, second))  43.5 us
    ppermute x24, starting transfers between devices, shift(): return lax.ppermute(value, 'src', shift_pairs(step, second))  36.8 us
    ppermute x7, starting transfers between devices, swap(): return lax.ppermute(value, 'src', [(s, s ^ 1) for s in range(32)])  15.6 us
    pallas_call x1, Pallas kernels, spread_sums(): pl.pallas_call(spread_kernel, out_shape=jax.ShapeDtypeStruct((16, TILE, w...  12.3 us
    pallas_call x1, Pallas kernels, gather_sums(): pl.pallas_call(gather_kernel, out_shape=(blocks, blocks), in_specs=[spec(...  12.1 us
    ppermute x6, waiting for transfers between devices, turn(): lax.ppermute(value, 'tgt', [(t, (t + step) % SIDE) for t in range(SIDE)])  9.03 us
    convert_element_type x10, other arithmetic, add(): return total.astype(BF16)  7.25 us
    pallas_call x1, Pallas kernels, weight_terms(): pl.pallas_call(weight_kernel, out_shape=(blocks, blocks), in_specs=[spec(...  6.74 us
  transfers between devices with their start and end apart: 37, of which 22 were waited for; matrix products, arithmetic and copies ran while one was open for 4% of the time, Pallas kernels for 2%

profile of v1, /device:TPU:1, one launch (start us, length us, event | category | flops | bytes accessed | tf_op | source)
XLA Modules:
  0.0 173.2 jit_solution(16591432446554951387)
XLA Ops:
  3.3 12.1 %gather_sums.1 = (bf16[16,384,256]{2,1,0:T(8,128)(2,1)}, bf16[16,384,256]{2,1,0:T(8,128)(2,1)}) custom-call(s32[4]{0:T(128)} %pad_add_fusion.place, s32[32]{0:T(128)} %owner_map.3, s32[192]{0:T(256)} %targets0.3, s32[96]{0:T(128)} %targets1.3, s32[48]{0:T(128)} %targets2.3, s32[192]{0:T(256)} %sources0.3, s32[96]{0:T(128)} %sources1.3, s32[48]{0:T(128)} %sources2.3, ...), custom_call_target="tpu_custom_call" | custom-call | tf_op jit(solution)/shard_map/gather_sums/pallas_call | solution.py:129
  15.4 2.4 %collective-permute-start = (bf16[16,384,256]{2,1,0:T(8,128)(2,1)}, bf16[16,384,256]{2,1,0:T(8,128)(2,1)S(1)}, u32[]{:S(2)}, u32[]{:S(2)}) collective-permute-start(bf16[16,384,256]{2,1,0:T(8,128)(2,1)} %get-tuple-element.13), channel_id=1, source_target_pairs={{0,4},{4,0},{8,12},{12,8},{16,20},{20,16},{24,28},{28,24},{32,36},... | collective-permute-start | bytes 9437192 | tf_op jit(solution)/shard_map/ppermute | solution.py:364
  17.8 5.5 %collective-permute-done = bf16[16,384,256]{2,1,0:T(8,128)(2,1)S(1)} collective-permute-done((bf16[16,384,256]{2,1,0:T(8,128)(2,1)}, bf16[16,384,256]{2,1,0:T(8,128)(2,1)S(1)}, u32[]{:S(2)}, u32[]{:S(2)}) %collective-permute-start) | collective-permute-done | bytes 3145760 | tf_op jit(solution)/shard_map/ppermute | solution.py:364
  23.3 1.1 add_convert_fusion.5
  24.4 6.4 %collective-permute-start.1 = (bf16[2,384,256]{2,1,0:T(8,128)(2,1)S(1)}, bf16[2,384,256]{2,1,0:T(8,128)(2,1)S(1)}, u32[]{:S(2)}, u32[]{:S(2)}) collective-permute-start(bf16[2,384,256]{2,1,0:T(8,128)(2,1)S(1)} %add_convert_fusion.5), channel_id=1, source_target_pairs={{0,32},{4,12},{8,40},{12,20},{16,48},{20,28},{24,56},{28,4},{32,64... | collective-permute-start | bytes 1179656 | tf_op jit(solution)/shard_map/ppermute | solution.py:360
  30.8 4.7 %collective-permute-done.1 = bf16[2,384,256]{2,1,0:T(8,128)(2,1)S(1)} collective-permute-done((bf16[2,384,256]{2,1,0:T(8,128)(2,1)S(1)}, bf16[2,384,256]{2,1,0:T(8,128)(2,1)S(1)}, u32[]{:S(2)}, u32[]{:S(2)}) %collective-permute-start.1) | collective-permute-done | bytes 393248 | tf_op jit(solution)/shard_map/ppermute | solution.py:360
  35.5 1.9 %add_convert_fusion.4 = (bf16[2,384,256]{2,1,0:T(8,128)(2,1)S(1)}, bf16[2,384,256]{2,1,0:T(8,128)(2,1)S(1)}, bf16[2,384,256]{2,1,0:T(8,128)(2,1)S(1)}, bf16[2,384,256]{2,1,0:T(8,128)(2,1)S(1)}) fusion(bf16[2,384,256]{2,1,0:T(8,128)(2,1)S(1)} %collective-permute-done.1, bf16[16,384,256]{2,1,0:T(8,128)(2,1)S(1)} %collective-permute-done, ...), kind=kLoop, calls=%fused_computation.7 | loop fusion | flops 3538944 | bytes 5111808 | tf_op jit(solution)/shard_map/convert_element_type | solution.py:371
  38.1 1.6 collective-permute-start.2
  39.8 5.3 %collective-permute-done.3 = bf16[2,384,256]{2,1,0:T(8,128)(2,1)S(1)} collective-permute-done((bf16[2,384,256]{2,1,0:T(8,128)(2,1)S(1)}, bf16[2,384,256]{2,1,0:T(8,128)(2,1)S(1)}, u32[]{:S(2)}, u32[]{:S(2)}) %collective-permute-start.3) | collective-permute-done | bytes 393248 | tf_op jit(solution)/shard_map/ppermute | solution.py:360
  45.1 1.2 add_convert_fusion
  46.3 1.2 collective-permute-start.4
  47.5 3.0 %collective-permute-done.2 = bf16[4,384,256]{2,1,0:T(8,128)(2,1)S(1)} collective-permute-done((bf16[4,384,256]{2,1,0:T(8,128)(2,1)S(1)}, bf16[4,384,256]{2,1,0:T(8,128)(2,1)S(1)}, u32[]{:S(2)}, u32[]{:S(2)}) %collective-permute-start.2) | collective-permute-done | bytes 786464 | tf_op jit(solution)/shard_map/ppermute | solution.py:360
  50.6 6.7 %collective-permute-done.4 = bf16[4,384,256]{2,1,0:T(8,128)(2,1)S(1)} collective-permute-done((bf16[4,384,256]{2,1,0:T(8,128)(2,1)S(1)}, bf16[4,384,256]{2,1,0:T(8,128)(2,1)S(1)}, u32[]{:S(2)}, u32[]{:S(2)}) %collective-permute-start.4) | collective-permute-done | bytes 786464 | tf_op jit(solution)/shard_map/ppermute | solution.py:360
  57.2 2.3 %add_convert_fusion.6 = (bf16[1,384,256]{2,1,0:T(8,128)(2,1)S(1)}, bf16[1,384,256]{2,1,0:T(8,128)(2,1)S(1)}, bf16[1,384,256]{2,1,0:T(8,128)(2,1)S(1)}, bf16[384,256]{1,0:T(8,128)(2,1)}) fusion(bf16[4,384,256]{2,1,0:T(8,128)(2,1)S(1)} %collective-permute-done.4, bf16[4,384,256]{2,1,0:T(8,128)(2,1)S(1)} %collective-permute-done.2, ...), kind=kLoop, calls=%fused_computation.9 | loop fusion | flops 3145728 | bytes 3932160 | tf_op jit(solution)/shard_map/convert.4
  59.6 1.6 collective-permute-start.7
  61.2 1.3 collective-permute-start.5
  62.5 1.9 %collective-permute-done.7 = bf16[192,256]{1,0:T(8,128)(2,1)S(1)} collective-permute-done((bf16[192,256]{1,0:T(8,128)(2,1)S(1)}, bf16[192,256]{1,0:T(8,128)(2,1)S(1)}, u32[]{:S(2)}, u32[]{:S(2)}) %collective-permute-start.7) | collective-permute-done | bytes 98336 | tf_op jit(solution)/shard_map/ppermute | solution.py:360
  64.5 2.2 %collective-permute-start.8 = (bf16[384,256]{1,0:T(8,128)(2,1)S(1)}, bf16[384,256]{1,0:T(8,128)(2,1)S(1)}, u32[]{:S(2)}, u32[]{:S(2)}) collective-permute-start(bf16[384,256]{1,0:T(8,128)(2,1)S(1)} %pad_maximum_fusion.4), channel_id=1, source_target_pairs={{0,24},{4,100},{8,0},{12,108},{16,8},{20,116},{24,16},{28,124},{32... | collective-permute-start | bytes 589832 | tf_op jit(solution)/shard_map/ppermute | solution.py:360
  67.1 2.4 %collective-permute-done.8.part2 = bf16[384,256]{1,0:T(8,128)(2,1)S(1)} collective-permute-done((bf16[384,256]{1,0:T(8,128)(2,1)S(1)}, bf16[384,256]{1,0:T(8,128)(2,1)S(1)}, u32[]{:S(2)}, u32[]{:S(2)}) %collective-permute-start.8) | collective-permute-done | bytes 196640 | tf_op jit(solution)/shard_map/ppermute | solution.py:360
  69.5 3.3 %collective-permute-done.6.part1 = bf16[384,256]{1,0:T(8,128)(2,1)S(1)} collective-permute-done((bf16[384,256]{1,0:T(8,128)(2,1)S(1)}, bf16[384,256]{1,0:T(8,128)(2,1)S(1)}, u32[]{:S(2)}, u32[]{:S(2)}) %collective-permute-start.6) | collective-permute-done | bytes 196640 | tf_op jit(solution)/shard_map/ppermute | solution.py:360
  73.5 2.8 %hidden_terms.1 = (bf16[384,256]{1,0:T(8,128)(2,1)}, f32[128,256]{1,0:T(8,128)}, bf16[128,256]{1,0:T(8,128)(2,1)}, bf16[128,256]{1,0:T(8,128)(2,1)}, bf16[128,256]{1,0:T(8,128)(2,1)}) custom-call(s32[4]{0:T(128)} %pad_add_fusion.place, bf16[384,256]{1,0:T(8,128)(2,1)} %get-tuple-element.27.part0, bf16[384,256]{1,0:T(8,128)(2,1)} %copy-done.11, ...), custom_call_target="tpu_custom_call" | custom-call | tf_op jit(solution)/shard_map/hidden_terms/pallas_call | solution.py:269
  76.3 2.9 %collective-permute-start.10 = (bf16[128,256]{1,0:T(8,128)(2,1)}, bf16[128,256]{1,0:T(8,128)(2,1)S(1)}, u32[]{:S(2)}, u32[]{:S(2)}) collective-permute-start(bf16[128,256]{1,0:T(8,128)(2,1)} %get-tuple-element.16), channel_id=1, source_target_pairs={{0,2},{1,3},{2,0},{3,1},{4,6},{5,7},{6,4},{7,5},{8,10},{9,11},{10,... | collective-permute-start | bytes 196616 | tf_op jit(solution)/shard_map/ppermute | solution.py:401
  81.1 1.4 collective-permute-done.11
  82.5 2.0 %collective-permute-done.9 = bf16[128,256]{1,0:T(8,128)(2,1)S(1)} collective-permute-done((bf16[128,256]{1,0:T(8,128)(2,1)}, bf16[128,256]{1,0:T(8,128)(2,1)S(1)}, u32[]{:S(2)}, u32[]{:S(2)}) %collective-permute-start.9) | collective-permute-done | bytes 65568 | tf_op jit(solution)/shard_map/ppermute | solution.py:401
  84.5 1.7 fusion.5
  86.2 1.2 collective-permute-start.13
  87.7 2.1 %collective-permute-done.12.grad1 = bf16[128,256]{1,0:T(8,128)(2,1)S(1)} collective-permute-done((bf16[128,256]{1,0:T(8,128)(2,1)S(1)}, bf16[128,256]{1,0:T(8,128)(2,1)S(1)}, u32[]{:S(2)}, u32[]{:S(2)}) %collective-permute-start.12) | collective-permute-done | bytes 65568 | tf_op jit(solution)/shard_map/ppermute | solution.py:401
  89.7 1.6 collective-permute-done.13.grad2
  91.3 1.5 collective-permute-done.14.grad3
  93.5 6.7 %weight_terms.1 = (bf16[16,32,768]{2,1,0:T(8,128)(2,1)}, bf16[16,32,768]{2,1,0:T(8,128)(2,1)}) custom-call(s32[4]{0:T(128)} %pad_add_fusion.place, bf16[128,256]{1,0:T(8,128)(2,1)} %copy-done.6, bf16[128,256]{1,0:T(8,128)(2,1)} %copy-done.7, bf16[128,256]{1,0:T(8,128)(2,1)} %copy-done.8, bf16[128,256]{1,0:T(8,128)(2,1)} %copy-done.9, ...), custom_call_target="tpu_custom_call" | custom-call | tf_op jit(solution)/shard_map/weight_terms/pallas_call | solution.py:338
  100.2 9.3 %collective-permute-start.15 = (bf16[16,32,768]{2,1,0:T(8,128)(2,1)}, bf16[16,32,768]{2,1,0:T(8,128)(2,1)S(1)}, u32[]{:S(2)}, u32[]{:S(2)}) collective-permute-start(bf16[16,32,768]{2,1,0:T(8,128)(2,1)} %get-tuple-element.20), channel_id=1, source_target_pairs={{0,4},{4,0},{8,12},{12,8},{16,20},{20,16},{24,28},{28,24},{32,36},... | collective-permute-start | bytes 2359304 | tf_op jit(solution)/shard_map/ppermute | solution.py:364
  109.5 2.8 %form_messages.1 = bf16[768,128]{1,0:T(8,128)(2,1)} custom-call(s32[4]{0:T(128)} %pad_add_fusion.place, bf16[128,256]{1,0:T(8,128)(2,1)} %copy-done.6, bf16[128,256]{1,0:T(8,128)(2,1)} %copy-done.7, bf16[128,256]{1,0:T(8,128)(2,1)} %copy-done.8, bf16[128,256]{1,0:T(8,128)(2,1)} %copy-done.9, bf16[3,256,1024]{2,1,0:T(8,128)(2,1)} %weights.3), custom_call_target="tpu_custom_call" | custom-call | tf_op jit(solution)/shard_map/form_messages/pallas_call | solution.py:300
  112.4 2.7 %collective-permute-start.24 = (bf16[768,128]{1,0:T(8,128)(2,1)}, bf16[768,128]{1,0:T(8,128)(2,1)S(1)}, u32[]{:S(2)}, u32[]{:S(2)}) collective-permute-start(bf16[768,128]{1,0:T(8,128)(2,1)} %form_messages.1), channel_id=1, source_target_pairs={{0,96},{4,28},{8,104},{12,4},{16,112},{20,12},{24,120},{28,20},{32... | collective-permute-start | bytes 589832 | tf_op jit(solution)/shard_map/ppermute | solution.py:360
  116.1 2.5 %collective-permute-done.25 = bf16[768,128]{1,0:T(8,128)(2,1)S(1)} collective-permute-done((bf16[768,128]{1,0:T(8,128)(2,1)}, bf16[768,128]{1,0:T(8,128)(2,1)S(1)}, u32[]{:S(2)}, u32[]{:S(2)}) %collective-permute-start.25) | collective-permute-done | bytes 196640 | tf_op jit(solution)/shard_map/ppermute | solution.py:360
  118.7 2.7 %collective-permute-start.27 = (bf16[384,128]{1,0:T(8,128)(2,1)S(1)}, bf16[384,128]{1,0:T(8,128)(2,1)S(1)}, u32[]{:S(2)}, u32[]{:S(2)}) collective-permute-start(bf16[384,128]{1,0:T(8,128)(2,1)S(1)} %slice.385), channel_id=1, source_target_pairs={{0,96},{4,28},{8,104},{12,4},{16,112},{20,12},{24,120},{28,20},{32... | collective-permute-start | bytes 294920 | tf_op jit(solution)/shard_map/ppermute | solution.py:360
  121.5 1.1 add_convert_fusion.14
  122.7 1.5 collective-permute-start.17
  124.2 1.9 %collective-permute-done.18 = bf16[2,32,768]{2,1,0:T(8,128)(2,1)S(1)} collective-permute-done((bf16[2,32,768]{2,1,0:T(8,128)(2,1)S(1)}, bf16[2,32,768]{2,1,0:T(8,128)(2,1)S(1)}, u32[]{:S(2)}, u32[]{:S(2)}) %collective-permute-start.18) | collective-permute-done | bytes 98336 | tf_op jit(solution)/shard_map/ppermute | solution.py:360
  127.1 1.3 collective-permute-start.19
  128.6 3.4 %collective-permute-start.29 = (bf16[4,768,128]{2,1,0:T(8,128)(2,1)S(1)}, bf16[4,768,128]{2,1,0:T(8,128)(2,1)S(1)}, u32[]{:S(2)}, u32[]{:S(2)}) collective-permute-start(bf16[4,768,128]{2,1,0:T(8,128)(2,1)S(1)} %pad_maximum_fusion.2.own0), channel_id=1, source_target_pairs={{0,24},{4,100},{8,0},{12,108},{16,8},{20,116},{24,16},{28,124},{32... | collective-permute-start | bytes 2359304 | tf_op jit(solution)/shard_map/ppermute | solution.py:360
  133.1 3.6 %collective-permute-start.22 = (bf16[16,768]{1,0:T(8,128)(2,1)S(1)}, bf16[16,768]{1,0:T(8,128)(2,1)S(1)}, u32[]{:S(2)}, u32[]{:S(2)}) collective-permute-start(bf16[16,768]{1,0:T(8,128)(2,1)S(1)} %get-tuple-element.44), channel_id=1, source_target_pairs={{0,24},{4,100},{8,0},{12,108},{16,8},{20,116},{24,16},{28,124},{32... | collective-permute-start | bytes 73736 | tf_op jit(solution)/shard_map/ppermute | solution.py:360
  136.7 5.2 %collective-permute-done.20 = bf16[16,768]{1,0:T(8,128)(2,1)S(1)} collective-permute-done((bf16[16,768]{1,0:T(8,128)(2,1)S(1)}, bf16[16,768]{1,0:T(8,128)(2,1)S(1)}, u32[]{:S(2)}, u32[]{:S(2)}) %collective-permute-start.20) | collective-permute-done | bytes 24608 | tf_op jit(solution)/shard_map/ppermute | solution.py:360
  142.0 1.3 collective-permute-done.22
  143.4 3.2 %collective-permute-start.23 = (bf16[32,768]{1,0:T(8,128)(2,1)S(1)}, bf16[32,768]{1,0:T(8,128)(2,1)S(1)}, u32[]{:S(2)}, u32[]{:S(2)}) collective-permute-start(bf16[32,768]{1,0:T(8,128)(2,1)S(1)} %pad_maximum_fusion.8), channel_id=1, source_target_pairs={{0,24},{4,100},{8,0},{12,108},{16,8},{20,116},{24,16},{28,124},{32... | collective-permute-start | bytes 147464 | tf_op jit(solution)/shard_map/ppermute | solution.py:360
  146.6 2.4 %collective-permute-start.32 = (bf16[4,768,128]{2,1,0:T(8,128)(2,1)S(1)}, bf16[4,768,128]{2,1,0:T(8,128)(2,1)S(1)}, u32[]{:S(2)}, u32[]{:S(2)}) collective-permute-start(bf16[4,768,128]{2,1,0:T(8,128)(2,1)S(1)} %pad_maximum_fusion.2.own0), channel_id=1, source_target_pairs={{0,4},{4,0},{8,12},{12,8},{16,20},{20,16},{24,28},{28,24},{32,36},... | collective-permute-start | bytes 2359304 | tf_op jit(solution)/shard_map/ppermute | solution.py:364
  149.2 2.7 %collective-permute-start.31 = (bf16[2,768,128]{2,1,0:T(8,128)(2,1)S(1)}, bf16[2,768,128]{2,1,0:T(8,128)(2,1)}, u32[]{:S(2)}, u32[]{:S(2)}) collective-permute-start(bf16[2,768,128]{2,1,0:T(8,128)(2,1)S(1)} %slice.387), channel_id=1, source_target_pairs={{0,24},{4,100},{8,0},{12,108},{16,8},{20,116},{24,16},{28,124},{32... | collective-permute-start | bytes 1179656 | tf_op jit(solution)/shard_map/ppermute | solution.py:360
  152.5 4.8 %collective-permute-done.30.own2a = bf16[2,768,128]{2,1,0:T(8,128)(2,1)} collective-permute-done((bf16[2,768,128]{2,1,0:T(8,128)(2,1)S(1)}, bf16[2,768,128]{2,1,0:T(8,128)(2,1)}, u32[]{:S(2)}, u32[]{:S(2)}) %collective-permute-start.30) | collective-permute-done | bytes 393248 | tf_op jit(solution)/shard_map/ppermute | solution.py:360
  160.7 12.3 %spread_sums.1 = bf16[16,128,256]{2,1,0:T(8,128)(2,1)} custom-call(s32[4]{0:T(128)} %pad_add_fusion.place, s32[32]{0:T(128)} %owner_map.3, s32[192]{0:T(256)} %targets0.3, s32[96]{0:T(128)} %targets1.3, s32[48]{0:T(128)} %targets2.3, s32[192]{0:T(256)} %sources0.3, s32[96]{0:T(128)} %sources1.3, s32[48]{0:T(128)} %sources2.3, s32[1]{0:T(128)S(6)} %copy.22.counts0, ...), custom_call_target="tpu_custom_call" | custom-call | tf_op jit(solution)/shard_map/spread_sums/pallas_call | solution.py:222
  (97 shorter events, 13.2 us)
Async XLA Ops:
  15.4 7.9 %collective-permute-start = (bf16[16,384,256]{2,1,0:T(8,128)(2,1)}, bf16[16,384,256]{2,1,0:T(8,128)(2,1)S(1)}, u32[]{:S(2)}, u32[]{:S(2)}) collective-permute-start(bf16[16,384,256]{2,1,0:T(8,128)(2,1)} %get-tuple-element.13), channel_id=1, source_target_pairs={{0,4},{4,0},{8,12},{12,8},{16,20},{20,16},{24,28},{28,24},{32,36},... | collective-permute-start | bytes 9437192 | tf_op jit(solution)/shard_map/ppermute | solution.py:364
  24.4 11.1 %collective-permute-start.1 = (bf16[2,384,256]{2,1,0:T(8,128)(2,1)S(1)}, bf16[2,384,256]{2,1,0:T(8,128)(2,1)S(1)}, u32[]{:S(2)}, u32[]{:S(2)}) collective-permute-start(bf16[2,384,256]{2,1,0:T(8,128)(2,1)S(1)} %add_convert_fusion.5), channel_id=1, source_target_pairs={{0,32},{4,12},{8,40},{12,20},{16,48},{20,28},{24,56},{28,4},{32,64... | collective-permute-start | bytes 1179656 | tf_op jit(solution)/shard_map/ppermute | solution.py:360
  37.4 7.7 %collective-permute-start.3 = (bf16[2,384,256]{2,1,0:T(8,128)(2,1)S(1)}, bf16[2,384,256]{2,1,0:T(8,128)(2,1)S(1)}, u32[]{:S(2)}, u32[]{:S(2)}) collective-permute-start(bf16[2,384,256]{2,1,0:T(8,128)(2,1)S(1)} %get-tuple-element.29), channel_id=1, source_target_pairs={{0,96},{4,28},{8,104},{12,4},{16,112},{20,12},{24,120},{28,20},{32... | collective-permute-start | bytes 1179656 | tf_op jit(solution)/shard_map/ppermute | solution.py:360
  38.1 12.4 %collective-permute-start.2 = (bf16[4,384,256]{2,1,0:T(8,128)(2,1)S(1)}, bf16[4,384,256]{2,1,0:T(8,128)(2,1)S(1)}, u32[]{:S(2)}, u32[]{:S(2)}) collective-permute-start(bf16[4,384,256]{2,1,0:T(8,128)(2,1)S(1)} %pad_maximum_fusion), channel_id=1, source_target_pairs={{0,32},{4,12},{8,40},{12,20},{16,48},{20,28},{24,56},{28,4},{32,64... | collective-permute-start | bytes 2359304 | tf_op jit(solution)/shard_map/ppermute | solution.py:360
  46.3 10.9 %collective-permute-start.4 = (bf16[4,384,256]{2,1,0:T(8,128)(2,1)S(1)}, bf16[4,384,256]{2,1,0:T(8,128)(2,1)S(1)}, u32[]{:S(2)}, u32[]{:S(2)}) collective-permute-start(bf16[4,384,256]{2,1,0:T(8,128)(2,1)S(1)} %pad_maximum_fusion.1), channel_id=1, source_target_pairs={{0,96},{4,28},{8,104},{12,4},{16,112},{20,12},{24,120},{28,20},{32... | collective-permute-start | bytes 2359304 | tf_op jit(solution)/shard_map/ppermute | solution.py:360
  59.6 21.1 %copy-start.13 = (bf16[256]{0:T(256)(128)(2,1)S(1)}, bf16[256]{0:T(256)(128)(2,1)}, u32[]{:S(2)}) copy-start(bf16[256]{0:T(256)(128)(2,1)} %param.32) | copy-start | bytes 1540
  59.6 24.9 %copy-start.12 = (bf16[128,256]{1,0:T(8,128)(2,1)S(1)}, bf16[128,256]{1,0:T(8,128)(2,1)}, u32[]{:S(2)}) copy-start(bf16[128,256]{1,0:T(8,128)(2,1)} %param.33) | copy-start | bytes 196612
  59.6 4.8 %collective-permute-start.7 = (bf16[192,256]{1,0:T(8,128)(2,1)S(1)}, bf16[192,256]{1,0:T(8,128)(2,1)S(1)}, u32[]{:S(2)}, u32[]{:S(2)}) collective-permute-start(bf16[192,256]{1,0:T(8,128)(2,1)S(1)} %get-tuple-element.41), channel_id=1, source_target_pairs={{0,24},{4,100},{8,0},{12,108},{16,8},{20,116},{24,16},{28,124},{32... | collective-permute-start | bytes 294920 | tf_op jit(solution)/shard_map/ppermute | solution.py:360
  61.2 5.7 %collective-permute-start.5 = (bf16[192,256]{1,0:T(8,128)(2,1)S(1)}, bf16[192,256]{1,0:T(8,128)(2,1)S(1)}, u32[]{:S(2)}, u32[]{:S(2)}) collective-permute-start(bf16[192,256]{1,0:T(8,128)(2,1)S(1)} %get-tuple-element.42), channel_id=1, source_target_pairs={{0,8},{4,36},{8,16},{12,44},{16,24},{20,52},{24,0},{28,60},{32,40}... | collective-permute-start | bytes 294920 | tf_op jit(solution)/shard_map/ppermute | solution.py:360
  64.5 5.0 %collective-permute-start.8 = (bf16[384,256]{1,0:T(8,128)(2,1)S(1)}, bf16[384,256]{1,0:T(8,128)(2,1)S(1)}, u32[]{:S(2)}, u32[]{:S(2)}) collective-permute-start(bf16[384,256]{1,0:T(8,128)(2,1)S(1)} %pad_maximum_fusion.4), channel_id=1, source_target_pairs={{0,24},{4,100},{8,0},{12,108},{16,8},{20,116},{24,16},{28,124},{32... | collective-permute-start | bytes 589832 | tf_op jit(solution)/shard_map/ppermute | solution.py:360
  67.0 5.8 %collective-permute-start.6 = (bf16[384,256]{1,0:T(8,128)(2,1)S(1)}, bf16[384,256]{1,0:T(8,128)(2,1)S(1)}, u32[]{:S(2)}, u32[]{:S(2)}) collective-permute-start(bf16[384,256]{1,0:T(8,128)(2,1)S(1)} %pad_maximum_fusion.3), channel_id=1, source_target_pairs={{0,8},{4,36},{8,16},{12,44},{16,24},{20,52},{24,0},{28,60},{32,40}... | collective-permute-start | bytes 589832 | tf_op jit(solution)/shard_map/ppermute | solution.py:360
  69.5 3.4 %copy-start.10 = (bf16[384,256]{1,0:T(8,128)(2,1)}, bf16[384,256]{1,0:T(8,128)(2,1)S(1)}, u32[]{:S(2)}) copy-start(bf16[384,256]{1,0:T(8,128)(2,1)S(1)} %collective-permute-done.8.part2) | copy-start | bytes 589828
  76.3 4.8 %collective-permute-start.10 = (bf16[128,256]{1,0:T(8,128)(2,1)}, bf16[128,256]{1,0:T(8,128)(2,1)S(1)}, u32[]{:S(2)}, u32[]{:S(2)}) collective-permute-start(bf16[128,256]{1,0:T(8,128)(2,1)} %get-tuple-element.16), channel_id=1, source_target_pairs={{0,2},{1,3},{2,0},{3,1},{4,6},{5,7},{6,4},{7,5},{8,10},{9,11},{10,... | collective-permute-start | bytes 196616 | tf_op jit(solution)/shard_map/ppermute | solution.py:401
  79.2 3.3 %collective-permute-start.11 = (bf16[128,256]{1,0:T(8,128)(2,1)}, bf16[128,256]{1,0:T(8,128)(2,1)S(1)}, u32[]{:S(2)}, u32[]{:S(2)}) collective-permute-start(bf16[128,256]{1,0:T(8,128)(2,1)} %get-tuple-element.17), channel_id=1, source_target_pairs={{0,3},{1,0},{2,1},{3,2},{4,7},{5,4},{6,5},{7,6},{8,11},{9,8},{10,9... | collective-permute-start | bytes 196616 | tf_op jit(solution)/shard_map/ppermute | solution.py:401
  80.0 4.5 %collective-permute-start.9 = (bf16[128,256]{1,0:T(8,128)(2,1)}, bf16[128,256]{1,0:T(8,128)(2,1)S(1)}, u32[]{:S(2)}, u32[]{:S(2)}) collective-permute-start(bf16[128,256]{1,0:T(8,128)(2,1)} %get-tuple-element.15), channel_id=1, source_target_pairs={{0,1},{1,2},{2,3},{3,0},{4,5},{5,6},{6,7},{7,4},{8,9},{9,10},{10,1... | collective-permute-start | bytes 196616 | tf_op jit(solution)/shard_map/ppermute | solution.py:401
  86.2 6.7 %copy-start.6 = (bf16[128,256]{1,0:T(8,128)(2,1)}, bf16[128,256]{1,0:T(8,128)(2,1)S(1)}, u32[]{:S(2)}) copy-start(bf16[128,256]{1,0:T(8,128)(2,1)S(1)} %get-tuple-element.39.grad0) | copy-start | bytes 196612
  86.2 3.5 %collective-permute-start.12 = (bf16[128,256]{1,0:T(8,128)(2,1)S(1)}, bf16[128,256]{1,0:T(8,128)(2,1)S(1)}, u32[]{:S(2)}, u32[]{:S(2)}) collective-permute-start(bf16[128,256]{1,0:T(8,128)(2,1)S(1)} %get-tuple-element.39.grad0), channel_id=1, source_target_pairs={{0,3},{1,0},{2,1},{3,2},{4,7},{5,4},{6,5},{7,6},{8,11},{9,8},{10,9... | collective-permute-start | bytes 196616 | tf_op jit(solution)/shard_map/ppermute | solution.py:401
  86.2 5.1 %collective-permute-start.13 = (bf16[128,256]{1,0:T(8,128)(2,1)S(1)}, bf16[128,256]{1,0:T(8,128)(2,1)S(1)}, u32[]{:S(2)}, u32[]{:S(2)}) collective-permute-start(bf16[128,256]{1,0:T(8,128)(2,1)S(1)} %get-tuple-element.39.grad0), channel_id=1, source_target_pairs={{0,2},{1,3},{2,0},{3,1},{4,6},{5,7},{6,4},{7,5},{8,10},{9,11},{10,... | collective-permute-start | bytes 196616 | tf_op jit(solution)/shard_map/ppermute | solution.py:401
  87.5 5.4 %collective-permute-start.14 = (bf16[128,256]{1,0:T(8,128)(2,1)S(1)}, bf16[128,256]{1,0:T(8,128)(2,1)S(1)}, u32[]{:S(2)}, u32[]{:S(2)}) collective-permute-start(bf16[128,256]{1,0:T(8,128)(2,1)S(1)} %get-tuple-element.39.grad0), channel_id=1, source_target_pairs={{0,1},{1,2},{2,3},{3,0},{4,5},{5,6},{6,7},{7,4},{8,9},{9,10},{10,1... | collective-permute-start | bytes 196616 | tf_op jit(solution)/shard_map/ppermute | solution.py:401
  89.7 3.1 %copy-start.7 = (bf16[128,256]{1,0:T(8,128)(2,1)}, bf16[128,256]{1,0:T(8,128)(2,1)S(1)}, u32[]{:S(2)}) copy-start(bf16[128,256]{1,0:T(8,128)(2,1)S(1)} %collective-permute-done.12.grad1) | copy-start | bytes 196612
  91.3 1.5 copy-start.8
  100.2 14.8 %collective-permute-start.15 = (bf16[16,32,768]{2,1,0:T(8,128)(2,1)}, bf16[16,32,768]{2,1,0:T(8,128)(2,1)S(1)}, u32[]{:S(2)}, u32[]{:S(2)}) collective-permute-start(bf16[16,32,768]{2,1,0:T(8,128)(2,1)} %get-tuple-element.20), channel_id=1, source_target_pairs={{0,4},{4,0},{8,12},{12,8},{16,20},{20,16},{24,28},{28,24},{32,36},... | collective-permute-start | bytes 2359304 | tf_op jit(solution)/shard_map/ppermute | solution.py:364
  112.4 16.1 %copy-start.4 = (bf16[768,128]{1,0:T(8,128)(2,1)S(1)}, bf16[768,128]{1,0:T(8,128)(2,1)}, u32[]{:S(2)}) copy-start(bf16[768,128]{1,0:T(8,128)(2,1)} %form_messages.1) | copy-start | bytes 589828
  112.4 6.2 %collective-permute-start.25 = (bf16[768,128]{1,0:T(8,128)(2,1)}, bf16[768,128]{1,0:T(8,128)(2,1)S(1)}, u32[]{:S(2)}, u32[]{:S(2)}) collective-permute-start(bf16[768,128]{1,0:T(8,128)(2,1)} %form_messages.1), channel_id=1, source_target_pairs={{0,32},{4,12},{8,40},{12,20},{16,48},{20,28},{24,56},{28,4},{32,64... | collective-permute-start | bytes 589832 | tf_op jit(solution)/shard_map/ppermute | solution.py:360
  112.4 6.3 %collective-permute-start.24 = (bf16[768,128]{1,0:T(8,128)(2,1)}, bf16[768,128]{1,0:T(8,128)(2,1)S(1)}, u32[]{:S(2)}, u32[]{:S(2)}) collective-permute-start(bf16[768,128]{1,0:T(8,128)(2,1)} %form_messages.1), channel_id=1, source_target_pairs={{0,96},{4,28},{8,104},{12,4},{16,112},{20,12},{24,120},{28,20},{32... | collective-permute-start | bytes 589832 | tf_op jit(solution)/shard_map/ppermute | solution.py:360
  115.1 28.3 %copy-start.5 = (bf16[16,32,768]{2,1,0:T(8,128)(2,1)}, bf16[16,32,768]{2,1,0:T(8,128)(2,1)S(1)}, u32[]{:S(2)}) copy-start(bf16[16,32,768]{2,1,0:T(8,128)(2,1)S(1)} %collective-permute-done.15) | copy-start | bytes 2359300
  116.0 5.4 %collective-permute-start.16 = (bf16[2,32,768]{2,1,0:T(8,128)(2,1)S(1)}, bf16[2,32,768]{2,1,0:T(8,128)(2,1)S(1)}, u32[]{:S(2)}, u32[]{:S(2)}) collective-permute-start(bf16[2,32,768]{2,1,0:T(8,128)(2,1)S(1)} %add_convert_fusion.15), channel_id=1, source_target_pairs={{0,32},{4,12},{8,40},{12,20},{16,48},{20,28},{24,56},{28,4},{32,64... | collective-permute-start | bytes 294920 | tf_op jit(solution)/shard_map/ppermute | solution.py:360
  118.6 9.8 %collective-permute-start.26 = (bf16[384,128]{1,0:T(8,128)(2,1)S(1)}, bf16[384,128]{1,0:T(8,128)(2,1)S(1)}, u32[]{:S(2)}, u32[]{:S(2)}) collective-permute-start(bf16[384,128]{1,0:T(8,128)(2,1)S(1)} %slice.384), channel_id=1, source_target_pairs={{0,32},{4,12},{8,40},{12,20},{16,48},{20,28},{24,56},{28,4},{32,64... | collective-permute-start | bytes 294920 | tf_op jit(solution)/shard_map/ppermute | solution.py:360
  118.7 9.7 %collective-permute-start.27 = (bf16[384,128]{1,0:T(8,128)(2,1)S(1)}, bf16[384,128]{1,0:T(8,128)(2,1)S(1)}, u32[]{:S(2)}, u32[]{:S(2)}) collective-permute-start(bf16[384,128]{1,0:T(8,128)(2,1)S(1)} %slice.385), channel_id=1, source_target_pairs={{0,96},{4,28},{8,104},{12,4},{16,112},{20,12},{24,120},{28,20},{32... | collective-permute-start | bytes 294920 | tf_op jit(solution)/shard_map/ppermute | solution.py:360
  122.6 3.5 %collective-permute-start.18 = (bf16[2,32,768]{2,1,0:T(8,128)(2,1)S(1)}, bf16[2,32,768]{2,1,0:T(8,128)(2,1)S(1)}, u32[]{:S(2)}, u32[]{:S(2)}) collective-permute-start(bf16[2,32,768]{2,1,0:T(8,128)(2,1)S(1)} %get-tuple-element.36), channel_id=1, source_target_pairs={{0,96},{4,28},{8,104},{12,4},{16,112},{20,12},{24,120},{28,20},{32... | collective-permute-start | bytes 294920 | tf_op jit(solution)/shard_map/ppermute | solution.py:360
  122.7 9.3 %collective-permute-start.17 = (bf16[4,32,768]{2,1,0:T(8,128)(2,1)S(1)}, bf16[4,32,768]{2,1,0:T(8,128)(2,1)S(1)}, u32[]{:S(2)}, u32[]{:S(2)}) collective-permute-start(bf16[4,32,768]{2,1,0:T(8,128)(2,1)S(1)} %pad_maximum_fusion.5), channel_id=1, source_target_pairs={{0,32},{4,12},{8,40},{12,20},{16,48},{20,28},{24,56},{28,4},{32,64... | collective-permute-start | bytes 589832 | tf_op jit(solution)/shard_map/ppermute | solution.py:360
  127.1 5.0 %collective-permute-start.19 = (bf16[4,32,768]{2,1,0:T(8,128)(2,1)S(1)}, bf16[4,32,768]{2,1,0:T(8,128)(2,1)S(1)}, u32[]{:S(2)}, u32[]{:S(2)}) collective-permute-start(bf16[4,32,768]{2,1,0:T(8,128)(2,1)S(1)} %pad_maximum_fusion.6), channel_id=1, source_target_pairs={{0,96},{4,28},{8,104},{12,4},{16,112},{20,12},{24,120},{28,20},{32... | collective-permute-start | bytes 589832 | tf_op jit(solution)/shard_map/ppermute | solution.py:360
  128.6 31.9 %copy-start = (bf16[4,768,128]{2,1,0:T(8,128)(2,1)}, bf16[4,768,128]{2,1,0:T(8,128)(2,1)S(1)}, u32[]{:S(2)}) copy-start(bf16[4,768,128]{2,1,0:T(8,128)(2,1)S(1)} %pad_maximum_fusion.2.own0) | copy-start | bytes 2359300
  128.6 20.4 %collective-permute-start.28 = (bf16[4,768,128]{2,1,0:T(8,128)(2,1)S(1)}, bf16[4,768,128]{2,1,0:T(8,128)(2,1)S(1)}, u32[]{:S(2)}, u32[]{:S(2)}) collective-permute-start(bf16[4,768,128]{2,1,0:T(8,128)(2,1)S(1)} %pad_maximum_fusion.2.own0), channel_id=1, source_target_pairs={{0,8},{4,36},{8,16},{12,44},{16,24},{20,52},{24,0},{28,60},{32,40}... | collective-permute-start | bytes 2359304 | tf_op jit(solution)/shard_map/ppermute | solution.py:360
  128.6 20.5 %collective-permute-start.29 = (bf16[4,768,128]{2,1,0:T(8,128)(2,1)S(1)}, bf16[4,768,128]{2,1,0:T(8,128)(2,1)S(1)}, u32[]{:S(2)}, u32[]{:S(2)}) collective-permute-start(bf16[4,768,128]{2,1,0:T(8,128)(2,1)S(1)} %pad_maximum_fusion.2.own0), channel_id=1, source_target_pairs={{0,24},{4,100},{8,0},{12,108},{16,8},{20,116},{24,16},{28,124},{32... | collective-permute-start | bytes 2359304 | tf_op jit(solution)/shard_map/ppermute | solution.py:360
  133.0 8.9 %collective-permute-start.20 = (bf16[16,768]{1,0:T(8,128)(2,1)S(1)}, bf16[16,768]{1,0:T(8,128)(2,1)S(1)}, u32[]{:S(2)}, u32[]{:S(2)}) collective-permute-start(bf16[16,768]{1,0:T(8,128)(2,1)S(1)} %get-tuple-element.43), channel_id=1, source_target_pairs={{0,8},{4,36},{8,16},{12,44},{16,24},{20,52},{24,0},{28,60},{32,40}... | collective-permute-start | bytes 73736 | tf_op jit(solution)/shard_map/ppermute | solution.py:360
  133.1 10.2 %collective-permute-start.22 = (bf16[16,768]{1,0:T(8,128)(2,1)S(1)}, bf16[16,768]{1,0:T(8,128)(2,1)S(1)}, u32[]{:S(2)}, u32[]{:S(2)}) collective-permute-start(bf16[16,768]{1,0:T(8,128)(2,1)S(1)} %get-tuple-element.44), channel_id=1, source_target_pairs={{0,24},{4,100},{8,0},{12,108},{16,8},{20,116},{24,16},{28,124},{32... | collective-permute-start | bytes 73736 | tf_op jit(solution)/shard_map/ppermute | solution.py:360
  141.9 9.9 %collective-permute-start.21 = (bf16[32,768]{1,0:T(8,128)(2,1)S(1)}, bf16[32,768]{1,0:T(8,128)(2,1)S(1)}, u32[]{:S(2)}, u32[]{:S(2)}) collective-permute-start(bf16[32,768]{1,0:T(8,128)(2,1)S(1)} %pad_maximum_fusion.7), channel_id=1, source_target_pairs={{0,8},{4,36},{8,16},{12,44},{16,24},{20,52},{24,0},{28,60},{32,40}... | collective-permute-start | bytes 147464 | tf_op jit(solution)/shard_map/ppermute | solution.py:360
  143.4 9.1 %collective-permute-start.23 = (bf16[32,768]{1,0:T(8,128)(2,1)S(1)}, bf16[32,768]{1,0:T(8,128)(2,1)S(1)}, u32[]{:S(2)}, u32[]{:S(2)}) collective-permute-start(bf16[32,768]{1,0:T(8,128)(2,1)S(1)} %pad_maximum_fusion.8), channel_id=1, source_target_pairs={{0,24},{4,100},{8,0},{12,108},{16,8},{20,116},{24,16},{28,124},{32... | collective-permute-start | bytes 147464 | tf_op jit(solution)/shard_map/ppermute | solution.py:360
  146.6 13.2 %collective-permute-start.32 = (bf16[4,768,128]{2,1,0:T(8,128)(2,1)S(1)}, bf16[4,768,128]{2,1,0:T(8,128)(2,1)S(1)}, u32[]{:S(2)}, u32[]{:S(2)}) collective-permute-start(bf16[4,768,128]{2,1,0:T(8,128)(2,1)S(1)} %pad_maximum_fusion.2.own0), channel_id=1, source_target_pairs={{0,4},{4,0},{8,12},{12,8},{16,20},{20,16},{24,28},{28,24},{32,36},... | collective-permute-start | bytes 2359304 | tf_op jit(solution)/shard_map/ppermute | solution.py:364
  149.0 11.5 %copy-start.1 = (bf16[4,768,128]{2,1,0:T(8,128)(2,1)}, bf16[4,768,128]{2,1,0:T(8,128)(2,1)S(1)}, u32[]{:S(2)}) copy-start(bf16[4,768,128]{2,1,0:T(8,128)(2,1)S(1)} %collective-permute-done.28.own3) | copy-start | bytes 2359300
  149.0 8.3 %collective-permute-start.30 = (bf16[2,768,128]{2,1,0:T(8,128)(2,1)S(1)}, bf16[2,768,128]{2,1,0:T(8,128)(2,1)}, u32[]{:S(2)}, u32[]{:S(2)}) collective-permute-start(bf16[2,768,128]{2,1,0:T(8,128)(2,1)S(1)} %slice.386), channel_id=1, source_target_pairs={{0,8},{4,36},{8,16},{12,44},{16,24},{20,52},{24,0},{28,60},{32,40}... | collective-permute-start | bytes 1179656 | tf_op jit(solution)/shard_map/ppermute | solution.py:360
  149.1 11.4 %copy-start.2 = (bf16[4,768,128]{2,1,0:T(8,128)(2,1)}, bf16[4,768,128]{2,1,0:T(8,128)(2,1)S(1)}, u32[]{:S(2)}) copy-start(bf16[4,768,128]{2,1,0:T(8,128)(2,1)S(1)} %collective-permute-done.29.own1) | copy-start | bytes 2359300
  149.2 9.0 %collective-permute-start.31 = (bf16[2,768,128]{2,1,0:T(8,128)(2,1)S(1)}, bf16[2,768,128]{2,1,0:T(8,128)(2,1)}, u32[]{:S(2)}, u32[]{:S(2)}) collective-permute-start(bf16[2,768,128]{2,1,0:T(8,128)(2,1)S(1)} %slice.387), channel_id=1, source_target_pairs={{0,24},{4,100},{8,0},{12,108},{16,8},{20,116},{24,16},{28,124},{32... | collective-permute-start | bytes 1179656 | tf_op jit(solution)/shard_map/ppermute | solution.py:360
  151.9 8.6 %collective-permute-start.33 = (bf16[4,768,128]{2,1,0:T(8,128)(2,1)S(1)}, bf16[4,768,128]{2,1,0:T(8,128)(2,1)}, u32[]{:S(2)}, u32[]{:S(2)}) collective-permute-start(bf16[4,768,128]{2,1,0:T(8,128)(2,1)S(1)} %collective-permute-done.28.own3), channel_id=1, source_target_pairs={{0,4},{4,0},{8,12},{12,8},{16,20},{20,16},{24,28},{28,24},{32,36},... | collective-permute-start | bytes 2359304 | tf_op jit(solution)/shard_map/ppermute | solution.py:364
  152.5 8.0 %collective-permute-start.34 = (bf16[4,768,128]{2,1,0:T(8,128)(2,1)S(1)}, bf16[4,768,128]{2,1,0:T(8,128)(2,1)}, u32[]{:S(2)}, u32[]{:S(2)}) collective-permute-start(bf16[4,768,128]{2,1,0:T(8,128)(2,1)S(1)} %collective-permute-done.29.own1), channel_id=1, source_target_pairs={{0,4},{4,0},{8,12},{12,8},{16,20},{20,16},{24,28},{28,24},{32,36},... | collective-permute-start | bytes 2359304 | tf_op jit(solution)/shard_map/ppermute | solution.py:364
  157.3 2.6 %collective-permute-start.35 = (bf16[2,768,128]{2,1,0:T(8,128)(2,1)}, bf16[2,768,128]{2,1,0:T(8,128)(2,1)}, u32[]{:S(2)}, u32[]{:S(2)}) collective-permute-start(bf16[2,768,128]{2,1,0:T(8,128)(2,1)} %collective-permute-done.30.own2a), channel_id=1, source_target_pairs={{0,4},{4,0},{8,12},{12,8},{16,20},{20,16},{24,28},{28,24},{32,36},... | collective-permute-start | bytes 1179656 | tf_op jit(solution)/shard_map/ppermute | solution.py:364
  158.2 2.3 %collective-permute-start.36 = (bf16[2,768,128]{2,1,0:T(8,128)(2,1)}, bf16[2,768,128]{2,1,0:T(8,128)(2,1)}, u32[]{:S(2)}, u32[]{:S(2)}) collective-permute-start(bf16[2,768,128]{2,1,0:T(8,128)(2,1)} %collective-permute-done.31.own2b), channel_id=1, source_target_pairs={{0,4},{4,0},{8,12},{12,8},{16,20},{20,16},{24,28},{28,24},{32,36},... | collective-permute-start | bytes 1179656 | tf_op jit(solution)/shard_map/ppermute | solution.py:364
  (3 other events, 2.2 us)

commit v2 on v1

v2 whole, which is shorter than its diff:
```python
import functools

import jax
import jax.numpy as jnp
from jax import lax
from jax.experimental import pallas as pl
from jax.experimental.pallas import tpu as pltpu
from jax.sharding import PartitionSpec as P

TILE = 128
SIDE = 4
GROUP = 8
BF16 = jnp.bfloat16
F32 = jnp.float32
MIB = 1024 * 1024
LOAD = 24
QUAD = 4
barrier = lax.optimization_barrier


def spec(space):
    return pl.BlockSpec(memory_space=space)


ANY, SMEM, VMEM = pl.ANY, pltpu.SMEM, pltpu.VMEM


def here():
    s = lax.axis_index("src")
    return s // 8, (s // 2) % SIDE, s % 2


def place_of(slot, mine):
    x, z, c = slot // 8, (slot // 2) % SIDE, slot % 2
    dx = (x - mine[0] + SIDE) % SIDE
    dz = (z - mine[1] + SIDE) % SIDE
    first = jnp.where(c == 0, dx, dz)
    second = jnp.where(c == 0, dz, dx)
    away = jnp.where(c == mine[2], 0, 16)
    return first, second, away


def each_load(tiles, counts, buffer, sems, bases, act):
    for number in range(3):
        def step(part, carry, number=number):
            offset = part * LOAD
            act(
                pltpu.make_async_copy(
                    tiles[number].at[pl.ds(offset, LOAD)],
                    buffer.at[pl.ds(bases[number] + offset, LOAD)],
                    sems.at[bases[number] // LOAD + part],
                )
            )
            return carry

        lax.fori_loop(0, (counts[number][0] + LOAD - 1) // LOAD, step, 0)


def gather_kernel(
    owner_map,
    targets0, targets1, targets2, sources0, sources1, sources2, counts0, counts1, counts2,
    features, tiles0, tiles1, tiles2,
    keep, send,
    buffer, total, staged, table, pending, pair_a, pair_b, pair_spot, tile_sems, out_sems,
):
    targets, sources = (targets0, targets1, targets2), (sources0, sources1, sources2)
    counts, tiles = (counts0, counts1, counts2), (tiles0, tiles1, tiles2)
    capacities = [t.shape[0] for t in tiles]
    bases = [0, capacities[0], capacities[0] + capacities[1]]
    blank = sum(capacities)
    each_load(tiles, counts, buffer, tile_sems, bases, lambda copy: copy.start())
    mine = here()
    buffer[blank] = jnp.zeros((TILE, TILE), BF16)

    def fill(slot, carry):
        first, second, away = place_of(slot, mine)
        table[owner_map[slot]] = (away + first * SIDE + second) * 3
        for number in range(3):
            pending[slot * 3 + number] = -1
            total[slot * 3 + number] = jnp.zeros(total.shape[1:], F32)
        return carry

    lax.fori_loop(0, 32, fill, 0)

    found = jnp.int32(0)
    for number in range(3):
        def match(group, found, number=number):
            for lane in range(GROUP):
                j = group * GROUP + lane
                live = j < counts[number][0]
                spot = table[targets[number][j]] + number
                code = (bases[number] + j) + sources[number][j] * 1024
                waiting = pending[spot]
                pair_a[found] = waiting
                pair_b[found] = code
                pair_spot[found] = spot
                hit = waiting >= 0
                pending[spot] = jnp.where(live, jnp.where(hit, -1, code), waiting)
                found = found + jnp.where(live & hit, 1, 0)
            return found

        found = lax.fori_loop(0, (counts[number][0] + GROUP - 1) // GROUP, match, found)

    def flush(group, found):
        for lane in range(GROUP):
            spot = group * GROUP + lane
            waiting = pending[spot]
            pair_a[found] = waiting
            pair_b[found] = blank
            pair_spot[found] = spot
            found = found + jnp.where(waiting >= 0, 1, 0)
        return found

    found = lax.fori_loop(0, 96 // GROUP, flush, found)
    for lane in range(GROUP):
        pair_a[found + lane] = blank
        pair_b[found + lane] = blank
        pair_spot[found + lane] = 96
    each_load(tiles, counts, buffer, tile_sems, bases, lambda copy: copy.wait())

    def add_group(group, carry):
        products = []
        for lane in range(GROUP):
            a, b = pair_a[group * GROUP + lane], pair_b[group * GROUP + lane]
            tile = jnp.concatenate([buffer[a & 1023], buffer[b & 1023]], axis=1)
            block = jnp.concatenate([features[a >> 10], features[b >> 10]], axis=0)
            products.append(jnp.dot(tile, block, preferred_element_type=F32))
        for lane in range(GROUP):
            total[pair_spot[group * GROUP + lane]] += products[lane]
        return carry

    lax.fori_loop(0, (found + GROUP - 1) // GROUP, add_group, 0)

    def out_copy(where, spot):
        target = keep if where == 0 else send
        return pltpu.make_async_copy(
            staged.at[where * 16 + spot], target.at[spot], out_sems.at[where * 16 + spot]
        )

    for where in (1, 0):
        def emit(spot, carry, where=where):
            for number in range(3):
                staged[where * 16 + spot, pl.ds(number * TILE, TILE), :] = total[
                    (where * 16 + spot) * 3 + number
                ].astype(BF16)
            out_copy(where, spot).start()
            return carry

        lax.fori_loop(0, 16, emit, 0)
    for where in (1, 0):
        def finish(spot, carry, where=where):
            out_copy(where, spot).wait()
            return carry

        lax.fori_loop(0, 16, finish, 0)


def flat_args(relations):
    return (
        *[relation[1] for relation in relations],
        *[relation[2] for relation in relations],
        *[relation[3] for relation in relations],
    )


def gather_sums(owner_map, relations, features):
    width = features.shape[-1]
    slots = sum(relation[0].shape[0] for relation in relations)
    blocks = jax.ShapeDtypeStruct((16, 3 * TILE, width), BF16)
    pairs = slots // 2 + 48 + 2 * GROUP
    return pl.pallas_call(
        gather_kernel,
        out_shape=(blocks, blocks),
        in_specs=[spec(SMEM)] * 10 + [spec(VMEM)] + [spec(ANY)] * 3,
        out_specs=(spec(ANY), spec(ANY)),
        scratch_shapes=[
            pltpu.VMEM((slots + 1, TILE, TILE), BF16),
            pltpu.VMEM((97, TILE, width), F32),
            pltpu.VMEM((32, 3 * TILE, width), BF16),
            pltpu.SMEM((32,), jnp.int32),
            pltpu.SMEM((96,), jnp.int32),
            pltpu.SMEM((pairs,), jnp.int32),
            pltpu.SMEM((pairs,), jnp.int32),
            pltpu.SMEM((pairs,), jnp.int32),
            pltpu.SemaphoreType.DMA((slots // LOAD,)),
            pltpu.SemaphoreType.DMA((32,)),
        ],
        compiler_params=pltpu.CompilerParams(vmem_limit_bytes=36 * MIB),
        cost_estimate=pl.CostEstimate(
            flops=3 * 10**9, bytes_accessed=18 * 10**6, transcendentals=0
        ),
        name="gather_sums",
    )(
        owner_map,
        *flat_args(relations),
        features.reshape(-1, TILE, width),
        *[relation[0] for relation in relations],
    )


def plan_kernel(
    owner_map,
    targets0, targets1, targets2, sources0, sources1, sources2, counts0, counts1, counts2,
    capacities,
    codes, starts, spots, amount,
    table, filled,
):
    targets, sources = (targets0, targets1, targets2), (sources0, sources1, sources2)
    counts = (counts0, counts1, counts2)
    bases = [0, capacities[0], capacities[0] + capacities[1]]
    blank = sum(capacities)
    room = blank + 16
    mine = here()

    def fill(slot, carry):
        first, second, away = place_of(slot, mine)
        table[owner_map[slot]] = (away + second * SIDE + first) * 3
        return carry

    lax.fori_loop(0, 32, fill, 0)
    for source in range(17):
        filled[source] = 0
    for number in range(3):
        def sort(group, carry, number=number):
            for lane in range(GROUP):
                j = group * GROUP + lane
                source = jnp.where(j < counts[number][0], sources[number][j], 16)
                at = filled[source]
                codes[source * room + at] = (
                    bases[number] + j + (table[targets[number][j]] + number) * 1024
                )
                filled[source] = at + 1
            return carry

        lax.fori_loop(0, (counts[number][0] + GROUP - 1) // GROUP, sort, 0)
    found = jnp.int32(0)
    for source in range(16):
        for lane in range(QUAD):
            codes[source * room + filled[source] + lane] = blank
        quads = (filled[source] + QUAD - 1) // QUAD

        def emit(quad, found, source=source):
            starts[found] = source * room + quad * QUAD
            spots[found] = source
            return found + 1

        found = lax.fori_loop(0, quads, emit, found)
    for lane in range(QUAD):
        codes[17 * room + lane] = blank
        starts[found + lane] = 17 * room
        spots[found + lane] = 16
    amount[0] = found


def plan_spread(owner_map, relations):
    capacities = [relation[0].shape[0] for relation in relations]
    slots = sum(capacities)
    quads = slots // QUAD + 16 + 2 * QUAD
    return pl.pallas_call(
        lambda *refs: plan_kernel(*refs[:10], capacities, *refs[10:]),
        out_shape=(
            jax.ShapeDtypeStruct((17 * (slots + 16) + QUAD,), jnp.int32),
            jax.ShapeDtypeStruct((quads,), jnp.int32),
            jax.ShapeDtypeStruct((quads,), jnp.int32),
            jax.ShapeDtypeStruct((1,), jnp.int32),
        ),
        in_specs=[spec(SMEM)] * 10,
        out_specs=tuple([spec(SMEM)] * 4),
        scratch_shapes=[pltpu.SMEM((32,), jnp.int32), pltpu.SMEM((17,), jnp.int32)],
        compiler_params=pltpu.CompilerParams(vmem_limit_bytes=MIB),
        cost_estimate=pl.CostEstimate(flops=10**9, bytes_accessed=10**6, transcendentals=0),
        name="plan_spread",
    )(owner_map, *flat_args(relations))


def spread_kernel(
    codes, starts, spots, amount, counts0, counts1, counts2,
    tiles0, tiles1, tiles2,
    own0, own2, own3, own1, sib0, sib2, sib3, sib1,
    out,
    buffer, messages, total, tile_sems, in_sems,
):
    counts, tiles = (counts0, counts1, counts2), (tiles0, tiles1, tiles2)
    capacities = [t.shape[0] for t in tiles]
    bases = [0, capacities[0], capacities[0] + capacities[1]]
    blank = sum(capacities)
    pieces = [
        (own0, 0), (own2, 8), (own3, 12), (own1, 4),
        (sib0, 16), (sib2, 24), (sib3, 28), (sib1, 20),
    ]
    copies = [
        pltpu.make_async_copy(piece, messages.at[pl.ds(at * 3, 12)], in_sems.at[number])
        for number, (piece, at) in enumerate(pieces)
    ]
    for copy in copies:
        copy.start()
    each_load(tiles, counts, buffer, tile_sems, bases, lambda copy: copy.start())
    buffer[blank] = jnp.zeros((TILE, TILE), BF16)

    def clear(block, carry):
        total[block] = jnp.zeros(total.shape[1:], F32)
        return carry

    lax.fori_loop(0, 16, clear, 0)
    for copy in copies:
        copy.wait()
    each_load(tiles, counts, buffer, tile_sems, bases, lambda copy: copy.wait())

    def add_group(group, carry):
        products = []
        for lane in range(QUAD):
            start = starts[group * QUAD + lane]
            marks = [codes[start + k] for k in range(QUAD)]
            block = jnp.concatenate([messages[mark >> 10] for mark in marks], axis=1)
            tile = jnp.concatenate([buffer[mark & 1023] for mark in marks], axis=0)
            products.append(jnp.dot(block, tile, preferred_element_type=F32))
        for lane in range(QUAD):
            total[spots[group * QUAD + lane]] += products[lane]
        return carry

    lax.fori_loop(0, (amount[0] + QUAD - 1) // QUAD, add_group, 0)

    def emit(block, carry):
        out[block] = total[block].T.astype(BF16)
        return carry

    lax.fori_loop(0, 16, emit, 0)


def spread_sums(plan, relations, pieces, width):
    slots = sum(relation[0].shape[0] for relation in relations)
    return pl.pallas_call(
        spread_kernel,
        out_shape=jax.ShapeDtypeStruct((16, TILE, width), BF16),
        in_specs=[spec(SMEM)] * 7 + [spec(ANY)] * 11,
        out_specs=spec(VMEM),
        scratch_shapes=[
            pltpu.VMEM((slots + 1, TILE, TILE), BF16),
            pltpu.VMEM((96, width, TILE), BF16),
            pltpu.VMEM((17, width, TILE), F32),
            pltpu.SemaphoreType.DMA((slots // LOAD,)),
            pltpu.SemaphoreType.DMA((8,)),
        ],
        compiler_params=pltpu.CompilerParams(vmem_limit_bytes=26 * MIB),
        cost_estimate=pl.CostEstimate(
            flops=3 * 10**9, bytes_accessed=18 * 10**6, transcendentals=0
        ),
        name="spread_sums",
    )(
        *plan,
        *[relation[3] for relation in relations],
        *[relation[0] for relation in relations],
        *pieces,
    )


def columns_at(step, width):
    column = (lax.axis_index("tgt") + step) % SIDE
    return pl.ds(pl.multiple_of(column * width, width), width)


def hidden_kernel(part0, part1, part2, part3, weights, rounded, terms0, terms1, terms2, terms3):
    width = part0.shape[1]
    whole = part0[...].astype(F32)
    for part in (part1, part2, part3):
        whole = whole + part[...].astype(F32)
    whole = whole.astype(BF16)
    rounded[...] = whole
    for step, terms in ((2, terms2), (1, terms1), (3, terms3), (0, terms0)):
        value = jnp.zeros(terms.shape, F32)
        for number in range(3):
            value += jnp.dot(
                whole[number * TILE:(number + 1) * TILE],
                weights[number, :, columns_at(step, width)],
                preferred_element_type=F32,
            )
        terms[...] = value.astype(terms.dtype)


def hidden_terms(parts, weights):
    width = parts[0].shape[1]
    return pl.pallas_call(
        hidden_kernel,
        out_shape=(
            jax.ShapeDtypeStruct((3 * TILE, width), BF16),
            jax.ShapeDtypeStruct((TILE, width), F32),
            jax.ShapeDtypeStruct((TILE, width), BF16),
            jax.ShapeDtypeStruct((TILE, width), BF16),
            jax.ShapeDtypeStruct((TILE, width), BF16),
        ),
        in_specs=[spec(VMEM)] * 5,
        out_specs=tuple([spec(VMEM)] * 5),
        compiler_params=pltpu.CompilerParams(vmem_limit_bytes=8 * MIB),
        name="hidden_terms",
    )(*parts, weights)


def message_kernel(grad0, grad1, grad2, grad3, weights, messages):
    width = grad0.shape[1]
    for number in range(3):
        value = jnp.zeros((width, TILE), F32)
        for step, grad in enumerate((grad0, grad1, grad2, grad3)):
            value += lax.dot_general(
                weights[number, :, columns_at(step, width)],
                grad[...],
                (((1,), (1,)), ((), ())),
                preferred_element_type=F32,
            )
        messages[number] = value.astype(BF16)


def form_messages(grads, weights):
    width = grads[0].shape[1]
    return pl.pallas_call(
        message_kernel,
        out_shape=jax.ShapeDtypeStruct((3, width, TILE), BF16),
        in_specs=[spec(VMEM)] * 5,
        out_specs=spec(VMEM),
        compiler_params=pltpu.CompilerParams(vmem_limit_bytes=8 * MIB),
        name="form_messages",
    )(*grads, weights)


def weight_kernel(grad0, grad1, grad2, grad3, rounded, keep, send, staged, sems):
    mine = here()
    block0 = lax.axis_index("tgt")
    values = jnp.concatenate(
        [rounded[number * TILE:(number + 1) * TILE, :] for number in range(3)], axis=1
    )
    for step, grad in enumerate((grad0, grad1, grad2, grad3)):
        turned = grad[...].astype(F32).T.astype(BF16)
        block = (block0 + step) % SIDE
        for part in range(8):
            first, second, away = place_of(block * 8 + part, mine)
            spot = away + second * SIDE + first
            value = jnp.dot(
                turned[part * 32:(part + 1) * 32], values, preferred_element_type=F32
            ).astype(BF16)
            for column in range(values.shape[1] // TILE):
                staged[spot, pl.ds(column * 32, 32), :] = value[
                    :, column * TILE:(column + 1) * TILE
                ]
    copies = [
        pltpu.make_async_copy(staged.at[pl.ds(16, 16)], send, sems.at[0]),
        pltpu.make_async_copy(staged.at[pl.ds(0, 16)], keep, sems.at[1]),
    ]
    for copy in copies:
        copy.start()
    for copy in copies:
        copy.wait()


def weight_terms(grads, rounded):
    width = grads[0].shape[1]
    rows = 32 * 3 * width // TILE
    blocks = jax.ShapeDtypeStruct((16, rows, TILE), BF16)
    return pl.pallas_call(
        weight_kernel,
        out_shape=(blocks, blocks),
        in_specs=[spec(VMEM)] * 5,
        out_specs=(spec(ANY), spec(ANY)),
        scratch_shapes=[
            pltpu.VMEM((32, rows, TILE), BF16),
            pltpu.SemaphoreType.DMA((2,)),
        ],
        compiler_params=pltpu.CompilerParams(vmem_limit_bytes=8 * MIB),
        cost_estimate=pl.CostEstimate(flops=10**9, bytes_accessed=3 * 10**6, transcendentals=0),
        name="weight_terms",
    )(*grads, rounded)


def shift_pairs(step, second):
    pairs = []
    for s in range(32):
        x, z, c = s // 8, (s // 2) % 4, s % 2
        if (c == 0) != second:
            x = (x + step) % SIDE
        else:
            z = (z + step) % SIDE
        pairs.append((s, (x * SIDE + z) * 2 + c))
    return pairs


def shift(value, step, second=False):
    return lax.ppermute(value, "src", shift_pairs(step, second))


def swap(value):
    return lax.ppermute(value, "src", [(s, s ^ 1) for s in range(32)])


def add(*values):
    total = values[0].astype(F32)
    for value in values[1:]:
        total = total + value.astype(F32)
    return total.astype(BF16)


def three_ways(values, second=False):
    return barrier(
        tuple(shift(values[k], k if k < 3 else -1, second) for k in (2, 1, 3))
    )


def turn(value, step):
    return lax.ppermute(value, "tgt", [(t, (t + step) % SIDE) for t in range(SIDE)])


def shards(
    features,
    cites_tiles,
    cites_targets,
    cites_sources,
    cites_counts,
    writes_tiles,
    writes_targets,
    writes_sources,
    writes_counts,
    topic_tiles,
    topic_targets,
    topic_sources,
    topic_counts,
    owner_map,
    weights,
    bias_row,
    cotangent,
):
    width = features.shape[1]
    relations = (
        (cites_tiles, cites_targets, cites_sources, cites_counts),
        (writes_tiles, writes_targets, writes_sources, writes_counts),
        (topic_tiles, topic_targets, topic_sources, topic_counts),
    )
    keep, send = gather_sums(owner_map, relations, features)
    got = swap(send)
    quarters = [add(keep[4 * k:4 * k + 4], got[4 * k:4 * k + 4]) for k in range(4)]
    arrived = three_ways(quarters)
    line = [add(quarters[0][k], *[part[k] for part in arrived]) for k in range(4)]
    owner_map, *line = barrier((owner_map, *line))
    plan = plan_spread(owner_map, relations)
    parts = (line[0], *three_ways(line, True))

    rounded, terms0, terms1, terms2, terms3 = hidden_terms(parts, weights)
    turned = barrier((turn(terms2, 2), turn(terms1, 1), turn(terms3, 3)))
    hidden = terms0 + bias_row.astype(F32)[None, :]
    for part in turned:
        hidden = hidden + part.astype(F32)
    mixed_out, pullback = jax.vjp(functools.partial(jax.nn.gelu, approximate=True), hidden)
    grad_hidden = pullback(cotangent.astype(F32))[0].astype(BF16)
    two, one, three = barrier(
        (turn(grad_hidden, -2), turn(grad_hidden, -1), turn(grad_hidden, -3))
    )
    grads = [grad_hidden, one, two, three]

    own = form_messages(grads, weights)
    held = (own, own, own, own)
    two, three, one = three_ways(held)
    weight_keep, weight_send = weight_terms(grads, rounded)
    weight_got = swap(weight_send)
    whole = jnp.concatenate([own, one, two, three])
    whole, weight_keep, weight_got = barrier((whole, weight_keep, weight_got))
    spread_out = (shift(whole, 2, True), shift(whole, 1, True), shift(whole, -1, True))
    beside = swap(whole)
    quarters = [
        add(weight_keep[4 * k:4 * k + 4], weight_got[4 * k:4 * k + 4]) for k in range(4)
    ]
    arrived = three_ways(quarters, True)
    line = [add(quarters[0][k], *[part[k] for part in arrived]) for k in range(4)]
    *spread_out, beside, l0, l1, l2, l3 = barrier((*spread_out, beside, *line))
    siblings = [swap(piece) for piece in spread_out]
    weight_parts = three_ways((l0, l1, l2, l3))
    grad_source = spread_sums(
        plan, relations, [whole, *spread_out, beside, *siblings], width
    )
    weight_sum = l0.astype(F32)
    for part in weight_parts:
        weight_sum = weight_sum + part.astype(F32)
    grad_weight = weight_sum.reshape(3 * width // TILE, 32, TILE).transpose(0, 2, 1)
    return (
        mixed_out.astype(BF16),
        grad_weight.reshape(3, width, 32),
        grad_source.reshape(-1, width),
    )


def solution(mesh):
    in_specs = (
        P("src", "tgt"),
        P("src", None, None),
        P("src"),
        P("src"),
        P("src"),
        P("src", None, None),
        P("src"),
        P("src"),
        P("src"),
        P("src", None, None),
        P("src"),
        P("src"),
        P("src"),
        P(),
        P(None, "tgt", None),
        P("tgt"),
        P("src", "tgt"),
    )
    out_specs = (P("src", "tgt"), P(None, "tgt", "src"), P("src", "tgt"))
    return jax.shard_map(shards, mesh=mesh, in_specs=in_specs, out_specs=out_specs, check_vma=False)
```

time: 176 us -> 174 us (0.989)
  the two profiles are of different devices: /device:TPU:1 before, /device:TPU:7 now
where the time goes in v2:
time: 174 us; the launch traced here: 175 us
  waiting for transfers between devices  60.1 us (35%)
  Pallas kernels  46.8 us (27%)
  starting transfers between devices  43.2 us (25%)
  local copies, waits for them, and re-layouts  19.2 us (11%)
  between operations  3.01 us (2%)
  other arithmetic  2.6 us (1%)
    ppermute x18, waiting for transfers between devices, shift(): return lax.ppermute(value, 'src', shift_pairs(step, second))  48.5 us
    pallas_call x1, Pallas kernels, gather_sums(): pl.pallas_call(gather_kernel, out_shape=(blocks, blocks), in_specs=[spec(...  23.2 us
    ppermute x18, starting transfers between devices, shift(): return lax.ppermute(value, 'src', shift_pairs(step, second))  21.1 us
    unnamed x43, local copies, waits for them, and re-layouts  19.1 us
    pallas_call x1, Pallas kernels, spread_sums(): pl.pallas_call(spread_kernel, out_shape=jax.ShapeDtypeStruct((16, TILE, w...  16.3 us
    ppermute x6, starting transfers between devices, swap(): return lax.ppermute(value, 'src', [(s, s ^ 1) for s in range(32)])  13.3 us
    ppermute x6, starting transfers between devices, turn(): lax.ppermute(value, 'tgt', [(t, (t + step) % SIDE) for t in range(SIDE)])  8.81 us
    ppermute x6, waiting for transfers between devices, turn(): lax.ppermute(value, 'tgt', [(t, (t + step) % SIDE) for t in range(SIDE)])  5.94 us
  transfers between devices with their start and end apart: 30, of which 14 were waited for; matrix products, arithmetic and copies ran while one was open for 1% of the time, Pallas kernels for 3%

profile of v2, /device:TPU:7, one launch (start us, length us, event | category | flops | bytes accessed | tf_op | source)
XLA Modules:
  0.0 174.8 jit_solution(7678447064366197478)
XLA Ops:
  2.6 2.8 %copy-done = bf16[192,128,128]{2,1,0:T(8,128)(2,1)S(1)} copy-done((bf16[192,128,128]{2,1,0:T(8,128)(2,1)S(1)}, bf16[192,128,128]{2,1,0:T(8,128)(2,1)}, u32[]{:S(2)}) %copy-start) | copy-done | bytes 6291480
  5.4 1.9 %copy-done.2 = bf16[96,128,128]{2,1,0:T(8,128)(2,1)S(1)} copy-done((bf16[96,128,128]{2,1,0:T(8,128)(2,1)S(1)}, bf16[96,128,128]{2,1,0:T(8,128)(2,1)}, u32[]{:S(2)}) %copy-start.2) | copy-done | bytes 3145752
  7.3 1.4 copy-done.5
  8.7 1.2 copy-done.9
  14.5 23.2 %gather_sums.1 = (bf16[16,384,256]{2,1,0:T(8,128)(2,1)S(1)}, bf16[16,384,256]{2,1,0:T(8,128)(2,1)S(1)}) custom-call(s32[32]{0:T(128)S(1)} %copy-done.14, s32[192]{0:T(256)S(1)} %copy-done.12, s32[96]{0:T(128)S(1)} %copy-done.15, s32[48]{0:T(128)S(1)} %copy-done.16, s32[192]{0:T(256)S(1)} %copy-done.13, s32[96]{0:T(128)S(1)} %copy-done.17, s32[48]{0:T(128)S(1)} %copy-done.18, ...), custom_call_target="tpu_custom_call" | custom-call | flops 3000000000 | bytes 18000000 | tf_op jit(solution)/shard_map/gather_sums/pallas_call | solution.py:171
  37.8 5.6 %collective-permute-done = bf16[16,384,256]{2,1,0:T(8,128)(2,1)S(1)} collective-permute-done((bf16[16,384,256]{2,1,0:T(8,128)(2,1)S(1)}, bf16[16,384,256]{2,1,0:T(8,128)(2,1)S(1)}, u32[]{:S(2)}, u32[]{:S(2)}) %collective-permute-start) | collective-permute-done | bytes 3145760 | tf_op jit(solution)/shard_map/ppermute | solution.py:489
  43.5 1.0 add_convert_fusion
  44.5 1.2 collective-permute-start.1
  45.7 2.7 %collective-permute-start.3 = (bf16[4,384,256]{2,1,0:T(8,128)(2,1)S(1)}, bf16[4,384,256]{2,1,0:T(8,128)(2,1)S(1)}, u32[]{:S(2)}, u32[]{:S(2)}) collective-permute-start(bf16[4,384,256]{2,1,0:T(8,128)(2,1)S(1)} %get-tuple-element.106), channel_id=1, source_target_pairs={{0,96},{4,28},{8,104},{12,4},{16,112},{20,12},{24,120},{28,20},{32... | collective-permute-start | bytes 2359304 | tf_op jit(solution)/shard_map/ppermute | solution.py:485
  48.4 8.8 %collective-permute-done.1 = bf16[4,384,256]{2,1,0:T(8,128)(2,1)S(1)} collective-permute-done((bf16[4,384,256]{2,1,0:T(8,128)(2,1)S(1)}, bf16[4,384,256]{2,1,0:T(8,128)(2,1)S(1)}, u32[]{:S(2)}, u32[]{:S(2)}) %collective-permute-start.1) | collective-permute-done | bytes 786464 | tf_op jit(solution)/shard_map/ppermute | solution.py:485
  57.2 8.4 %collective-permute-done.2 = bf16[4,384,256]{2,1,0:T(8,128)(2,1)S(1)} collective-permute-done((bf16[4,384,256]{2,1,0:T(8,128)(2,1)S(1)}, bf16[4,384,256]{2,1,0:T(8,128)(2,1)S(1)}, u32[]{:S(2)}, u32[]{:S(2)}) %collective-permute-start.2) | collective-permute-done | bytes 786464 | tf_op jit(solution)/shard_map/ppermute | solution.py:485
  66.0 1.4 collective-permute-start.4
  67.5 1.5 collective-permute-start.6
  68.9 3.5 %collective-permute-done.4.part1 = bf16[384,256]{1,0:T(8,128)(2,1)S(1)} collective-permute-done((bf16[384,256]{1,0:T(8,128)(2,1)S(1)}, bf16[384,256]{1,0:T(8,128)(2,1)S(1)}, u32[]{:S(2)}, u32[]{:S(2)}) %collective-permute-start.4) | collective-permute-done | bytes 196640 | tf_op jit(solution)/shard_map/ppermute | solution.py:485
  72.4 2.1 %collective-permute-done.6.part3 = bf16[384,256]{1,0:T(8,128)(2,1)S(1)} collective-permute-done((bf16[384,256]{1,0:T(8,128)(2,1)S(1)}, bf16[384,256]{1,0:T(8,128)(2,1)S(1)}, u32[]{:S(2)}, u32[]{:S(2)}) %collective-permute-start.6) | collective-permute-done | bytes 196640 | tf_op jit(solution)/shard_map/ppermute | solution.py:485
  75.0 3.0 %collective-permute-start.7 = (bf16[128,256]{1,0:T(8,128)(2,1)S(1)}, bf16[128,256]{1,0:T(8,128)(2,1)S(1)}, u32[]{:S(2)}, u32[]{:S(2)}) collective-permute-start(bf16[128,256]{1,0:T(8,128)(2,1)S(1)} %get-tuple-element.66), channel_id=1, source_target_pairs={{0,2},{1,3},{2,0},{3,1},{4,6},{5,7},{6,4},{7,5},{8,10},{9,11},{10,... | collective-permute-start | bytes 196616 | tf_op jit(solution)/shard_map/ppermute | solution.py:506
  78.4 2.3 %collective-permute-start.9 = (bf16[128,256]{1,0:T(8,128)(2,1)S(1)}, bf16[128,256]{1,0:T(8,128)(2,1)S(1)}, u32[]{:S(2)}, u32[]{:S(2)}) collective-permute-start(bf16[128,256]{1,0:T(8,128)(2,1)S(1)} %get-tuple-element.68), channel_id=1, source_target_pairs={{0,3},{1,0},{2,1},{3,2},{4,7},{5,4},{6,5},{7,6},{8,11},{9,8},{10,9... | collective-permute-start | bytes 196616 | tf_op jit(solution)/shard_map/ppermute | solution.py:506
  80.7 2.2 %collective-permute-done.8 = bf16[128,256]{1,0:T(8,128)(2,1)S(1)} collective-permute-done((bf16[128,256]{1,0:T(8,128)(2,1)S(1)}, bf16[128,256]{1,0:T(8,128)(2,1)S(1)}, u32[]{:S(2)}, u32[]{:S(2)}) %collective-permute-start.8) | collective-permute-done | bytes 65568 | tf_op jit(solution)/shard_map/ppermute | solution.py:506
  83.6 1.3 collective-permute-start.10
  84.9 1.3 collective-permute-start.11
  86.8 1.5 collective-permute-done.10.grad2
  88.2 0.9 collective-permute-done.11.grad1
  89.1 1.4 collective-permute-done.12.grad3
  90.5 1.2 weight_terms.1
  91.8 4.6 %collective-permute-start.16 = (bf16[16,192,128]{2,1,0:T(8,128)(2,1)S(1)}, bf16[16,192,128]{2,1,0:T(8,128)(2,1)S(1)}, u32[]{:S(2)}, u32[]{:S(2)}) collective-permute-start(bf16[16,192,128]{2,1,0:T(8,128)(2,1)S(1)} %get-tuple-element.80), channel_id=1, source_target_pairs={{0,4},{4,0},{8,12},{12,8},{16,20},{20,16},{24,28},{28,24},{32,36},... | collective-permute-start | bytes 2359304 | tf_op jit(solution)/shard_map/ppermute | solution.py:489
  97.0 1.4 collective-permute-start.13
  98.4 1.4 collective-permute-start.14
  99.8 1.3 collective-permute-start.15
  101.1 2.3 %collective-permute-done.13 = bf16[3,256,128]{2,1,0:T(8,128)(2,1)S(1)} collective-permute-done((bf16[3,256,128]{2,1,0:T(8,128)(2,1)S(1)}, bf16[3,256,128]{2,1,0:T(8,128)(2,1)S(1)}, u32[]{:S(2)}, u32[]{:S(2)}) %collective-permute-start.13) | collective-permute-done | bytes 196640 | tf_op jit(solution)/shard_map/ppermute | solution.py:485
  103.4 2.1 %collective-permute-done.14 = bf16[3,256,128]{2,1,0:T(8,128)(2,1)S(1)} collective-permute-done((bf16[3,256,128]{2,1,0:T(8,128)(2,1)S(1)}, bf16[3,256,128]{2,1,0:T(8,128)(2,1)S(1)}, u32[]{:S(2)}, u32[]{:S(2)}) %collective-permute-start.14) | collective-permute-done | bytes 196640 | tf_op jit(solution)/shard_map/ppermute | solution.py:485
  105.8 1.6 collective-permute-start.21
  107.4 1.4 collective-permute-start.17
  109.2 1.1 collective-permute-start.19
  110.3 3.8 %collective-permute-start.20 = (bf16[12,256,128]{2,1,0:T(8,128)(2,1)S(1)}, bf16[12,256,128]{2,1,0:T(8,128)(2,1)S(1)}, u32[]{:S(2)}, u32[]{:S(2)}) collective-permute-start(bf16[12,256,128]{2,1,0:T(8,128)(2,1)S(1)} %pad_maximum_fusion.own0), channel_id=1, source_target_pairs={{0,4},{4,0},{8,12},{12,8},{16,20},{20,16},{24,28},{28,24},{32,36},... | collective-permute-start | bytes 2359304 | tf_op jit(solution)/shard_map/ppermute | solution.py:489
  114.2 15.1 %collective-permute-done.22 = bf16[4,192,128]{2,1,0:T(8,128)(2,1)S(1)} collective-permute-done((bf16[4,192,128]{2,1,0:T(8,128)(2,1)S(1)}, bf16[4,192,128]{2,1,0:T(8,128)(2,1)S(1)}, u32[]{:S(2)}, u32[]{:S(2)}) %collective-permute-start.22) | collective-permute-done | bytes 196640 | tf_op jit(solution)/shard_map/ppermute | solution.py:485
  129.3 2.0 %collective-permute-start.23 = (bf16[4,192,128]{2,1,0:T(8,128)(2,1)S(1)}, bf16[4,192,128]{2,1,0:T(8,128)(2,1)S(1)}, u32[]{:S(2)}, u32[]{:S(2)}) collective-permute-start(bf16[4,192,128]{2,1,0:T(8,128)(2,1)S(1)} %get-tuple-element.114), channel_id=1, source_target_pairs={{0,24},{4,100},{8,0},{12,108},{16,8},{20,116},{24,16},{28,124},{32... | collective-permute-start | bytes 589832 | tf_op jit(solution)/shard_map/ppermute | solution.py:485
  131.3 3.8 %collective-permute-done.23 = bf16[4,192,128]{2,1,0:T(8,128)(2,1)S(1)} collective-permute-done((bf16[4,192,128]{2,1,0:T(8,128)(2,1)S(1)}, bf16[4,192,128]{2,1,0:T(8,128)(2,1)S(1)}, u32[]{:S(2)}, u32[]{:S(2)}) %collective-permute-start.23) | collective-permute-done | bytes 196640 | tf_op jit(solution)/shard_map/ppermute | solution.py:485
  135.2 4.2 %collective-permute-start.27 = (bf16[12,256,128]{2,1,0:T(8,128)(2,1)}, bf16[12,256,128]{2,1,0:T(8,128)(2,1)}, u32[]{:S(2)}, u32[]{:S(2)}) collective-permute-start(bf16[12,256,128]{2,1,0:T(8,128)(2,1)} %collective-permute-done.17.own2), channel_id=1, source_target_pairs={{0,4},{4,0},{8,12},{12,8},{16,20},{20,16},{24,28},{28,24},{32,36},... | collective-permute-start | bytes 2359304 | tf_op jit(solution)/shard_map/ppermute | solution.py:489
  140.0 1.3 collective-permute-start.24
  141.3 0.8 collective-permute-start.25
  142.1 2.3 %collective-permute-done.24 = bf16[192,128]{1,0:T(8,128)(2,1)S(1)} collective-permute-done((bf16[192,128]{1,0:T(8,128)(2,1)S(1)}, bf16[192,128]{1,0:T(8,128)(2,1)S(1)}, u32[]{:S(2)}, u32[]{:S(2)}) %collective-permute-start.24) | collective-permute-done | bytes 49184 | tf_op jit(solution)/shard_map/ppermute | solution.py:485
  144.4 1.5 collective-permute-start.26
  146.0 5.0 %plan_spread.1 = (s32[5988]{0:T(1024)S(1)}, s32[108]{0:T(128)S(1)}, s32[108]{0:T(128)S(1)}, s32[1]{0:T(128)}) custom-call(s32[32]{0:T(128)S(1)} %copy-done.14, s32[192]{0:T(256)S(1)} %copy-done.12, s32[96]{0:T(128)S(1)} %copy-done.15, s32[48]{0:T(128)S(1)} %copy-done.16, s32[192]{0:T(256)S(1)} %copy-done.13, s32[96]{0:T(128)S(1)} %copy-done.17, ...), custom_call_target="tpu_custom_call" | custom-call | flops 1000000000 | bytes 1000000 | tf_op jit(solution)/shard_map/plan_spread/pallas_call | solution.py:259
  151.9 2.8 %copy-done.1 = bf16[192,128,128]{2,1,0:T(8,128)(2,1)S(1)} copy-done((bf16[192,128,128]{2,1,0:T(8,128)(2,1)S(1)}, bf16[192,128,128]{2,1,0:T(8,128)(2,1)}, u32[]{:S(2)}) %copy-start.1) | copy-done | bytes 6291480
  154.7 1.4 copy-done.6
  156.1 1.1 copy-done.8
  157.2 1.1 copy-done.11
  158.3 16.3 %spread_sums.1 = bf16[16,128,256]{2,1,0:T(8,128)(2,1)} custom-call(s32[5988]{0:T(1024)S(1)} %get-tuple-element.95.codes, s32[108]{0:T(128)S(1)} %get-tuple-element.96.starts, s32[108]{0:T(128)S(1)} %get-tuple-element.97.spots, s32[1]{0:T(128)} %get-tuple-element.98.amount, s32[1]{0:T(128)S(6)} %copy.24.counts0.refs_7_, s32[1]{0:T(128)S(6)} %copy.25.counts1.refs_8_, ...), custom_call_target="tpu_custom_call" | custom-call | flops 3000000000 | bytes 18000000 | tf_op jit(solution)/shard_map/spread_sums/pallas_call | solution.py:332
  (71 shorter events, 10.1 us)
Async XLA Ops:
  2.6 2.8 %copy-start = (bf16[192,128,128]{2,1,0:T(8,128)(2,1)S(1)}, bf16[192,128,128]{2,1,0:T(8,128)(2,1)}, u32[]{:S(2)}) copy-start(bf16[192,128,128]{2,1,0:T(8,128)(2,1)} %tiles0.3) | copy-start | bytes 18874372
  5.4 1.9 %copy-start.2 = (bf16[96,128,128]{2,1,0:T(8,128)(2,1)S(1)}, bf16[96,128,128]{2,1,0:T(8,128)(2,1)}, u32[]{:S(2)}) copy-start(bf16[96,128,128]{2,1,0:T(8,128)(2,1)} %tiles1.3) | copy-start | bytes 9437188
  7.2 1.4 copy-start.5
  8.7 1.2 copy-start.9
  9.9 0.7 copy-start.12
  10.6 0.7 copy-start.13
  11.2 0.7 copy-start.14
  13.9 0.7 copy-start.18
  37.7 5.7 %collective-permute-start = (bf16[16,384,256]{2,1,0:T(8,128)(2,1)S(1)}, bf16[16,384,256]{2,1,0:T(8,128)(2,1)S(1)}, u32[]{:S(2)}, u32[]{:S(2)}) collective-permute-start(bf16[16,384,256]{2,1,0:T(8,128)(2,1)S(1)} %get-tuple-element.54), channel_id=1, source_target_pairs={{0,4},{4,0},{8,12},{12,8},{16,20},{20,16},{24,28},{28,24},{32,36},... | collective-permute-start | bytes 9437192 | tf_op jit(solution)/shard_map/ppermute | solution.py:489
  44.5 12.8 %collective-permute-start.1 = (bf16[4,384,256]{2,1,0:T(8,128)(2,1)S(1)}, bf16[4,384,256]{2,1,0:T(8,128)(2,1)S(1)}, u32[]{:S(2)}, u32[]{:S(2)}) collective-permute-start(bf16[4,384,256]{2,1,0:T(8,128)(2,1)S(1)} %get-tuple-element.108), channel_id=1, source_target_pairs={{0,64},{4,20},{8,72},{12,28},{16,80},{20,4},{24,88},{28,12},{32,96... | collective-permute-start | bytes 2359304 | tf_op jit(solution)/shard_map/ppermute | solution.py:485
  45.7 19.9 %collective-permute-start.2 = (bf16[4,384,256]{2,1,0:T(8,128)(2,1)S(1)}, bf16[4,384,256]{2,1,0:T(8,128)(2,1)S(1)}, u32[]{:S(2)}, u32[]{:S(2)}) collective-permute-start(bf16[4,384,256]{2,1,0:T(8,128)(2,1)S(1)} %get-tuple-element.107), channel_id=1, source_target_pairs={{0,32},{4,12},{8,40},{12,20},{16,48},{20,28},{24,56},{28,4},{32,64... | collective-permute-start | bytes 2359304 | tf_op jit(solution)/shard_map/ppermute | solution.py:485
  45.7 19.9 %collective-permute-start.3 = (bf16[4,384,256]{2,1,0:T(8,128)(2,1)S(1)}, bf16[4,384,256]{2,1,0:T(8,128)(2,1)S(1)}, u32[]{:S(2)}, u32[]{:S(2)}) collective-permute-start(bf16[4,384,256]{2,1,0:T(8,128)(2,1)S(1)} %get-tuple-element.106), channel_id=1, source_target_pairs={{0,96},{4,28},{8,104},{12,4},{16,112},{20,12},{24,120},{28,20},{32... | collective-permute-start | bytes 2359304 | tf_op jit(solution)/shard_map/ppermute | solution.py:485
  65.6 8.9 %copy-start.4 = (bf16[3,256,1024]{2,1,0:T(8,128)(2,1)S(1)}, bf16[3,256,1024]{2,1,0:T(8,128)(2,1)}, u32[]{:S(2)}) copy-start(bf16[3,256,1024]{2,1,0:T(8,128)(2,1)} %weights.3) | copy-start | bytes 4718596
  66.0 14.6 %copy-start.20 = (bf16[256]{0:T(256)(128)(2,1)S(1)}, bf16[256]{0:T(256)(128)(2,1)}, u32[]{:S(2)}) copy-start(bf16[256]{0:T(256)(128)(2,1)} %param.32) | copy-start | bytes 1540
  66.0 16.8 %copy-start.19 = (bf16[128,256]{1,0:T(8,128)(2,1)S(1)}, bf16[128,256]{1,0:T(8,128)(2,1)}, u32[]{:S(2)}) copy-start(bf16[128,256]{1,0:T(8,128)(2,1)} %param.33) | copy-start | bytes 196612
  66.0 6.4 %collective-permute-start.4 = (bf16[384,256]{1,0:T(8,128)(2,1)S(1)}, bf16[384,256]{1,0:T(8,128)(2,1)S(1)}, u32[]{:S(2)}, u32[]{:S(2)}) collective-permute-start(bf16[384,256]{1,0:T(8,128)(2,1)S(1)} %get-tuple-element.59), channel_id=1, source_target_pairs={{0,16},{4,68},{8,24},{12,76},{16,0},{20,84},{24,8},{28,92},{32,48}... | collective-permute-start | bytes 589832 | tf_op jit(solution)/shard_map/ppermute | solution.py:485
  67.5 5.0 %collective-permute-start.5 = (bf16[384,256]{1,0:T(8,128)(2,1)S(1)}, bf16[384,256]{1,0:T(8,128)(2,1)S(1)}, u32[]{:S(2)}, u32[]{:S(2)}) collective-permute-start(bf16[384,256]{1,0:T(8,128)(2,1)S(1)} %get-tuple-element.60), channel_id=1, source_target_pairs={{0,8},{4,36},{8,16},{12,44},{16,24},{20,52},{24,0},{28,60},{32,40}... | collective-permute-start | bytes 589832 | tf_op jit(solution)/shard_map/ppermute | solution.py:485
  67.5 7.1 %collective-permute-start.6 = (bf16[384,256]{1,0:T(8,128)(2,1)S(1)}, bf16[384,256]{1,0:T(8,128)(2,1)S(1)}, u32[]{:S(2)}, u32[]{:S(2)}) collective-permute-start(bf16[384,256]{1,0:T(8,128)(2,1)S(1)} %get-tuple-element.61), channel_id=1, source_target_pairs={{0,24},{4,100},{8,0},{12,108},{16,8},{20,116},{24,16},{28,124},{32... | collective-permute-start | bytes 589832 | tf_op jit(solution)/shard_map/ppermute | solution.py:485
  75.0 5.7 %collective-permute-start.7 = (bf16[128,256]{1,0:T(8,128)(2,1)S(1)}, bf16[128,256]{1,0:T(8,128)(2,1)S(1)}, u32[]{:S(2)}, u32[]{:S(2)}) collective-permute-start(bf16[128,256]{1,0:T(8,128)(2,1)S(1)} %get-tuple-element.66), channel_id=1, source_target_pairs={{0,2},{1,3},{2,0},{3,1},{4,6},{5,7},{6,4},{7,5},{8,10},{9,11},{10,... | collective-permute-start | bytes 196616 | tf_op jit(solution)/shard_map/ppermute | solution.py:506
  78.0 4.9 %collective-permute-start.8 = (bf16[128,256]{1,0:T(8,128)(2,1)S(1)}, bf16[128,256]{1,0:T(8,128)(2,1)S(1)}, u32[]{:S(2)}, u32[]{:S(2)}) collective-permute-start(bf16[128,256]{1,0:T(8,128)(2,1)S(1)} %get-tuple-element.67), channel_id=1, source_target_pairs={{0,1},{1,2},{2,3},{3,0},{4,5},{5,6},{6,7},{7,4},{8,9},{9,10},{10,1... | collective-permute-start | bytes 196616 | tf_op jit(solution)/shard_map/ppermute | solution.py:506
  78.4 4.5 %collective-permute-start.9 = (bf16[128,256]{1,0:T(8,128)(2,1)S(1)}, bf16[128,256]{1,0:T(8,128)(2,1)S(1)}, u32[]{:S(2)}, u32[]{:S(2)}) collective-permute-start(bf16[128,256]{1,0:T(8,128)(2,1)S(1)} %get-tuple-element.68), channel_id=1, source_target_pairs={{0,3},{1,0},{2,1},{3,2},{4,7},{5,4},{6,5},{7,6},{8,11},{9,8},{10,9... | collective-permute-start | bytes 196616 | tf_op jit(solution)/shard_map/ppermute | solution.py:506
  83.6 4.6 %collective-permute-start.10 = (bf16[128,256]{1,0:T(8,128)(2,1)S(1)}, bf16[128,256]{1,0:T(8,128)(2,1)S(1)}, u32[]{:S(2)}, u32[]{:S(2)}) collective-permute-start(bf16[128,256]{1,0:T(8,128)(2,1)S(1)} %get-tuple-element.122.grad0), channel_id=1, source_target_pairs={{0,2},{1,3},{2,0},{3,1},{4,6},{5,7},{6,4},{7,5},{8,10},{9,11},{10,... | collective-permute-start | bytes 196616 | tf_op jit(solution)/shard_map/ppermute | solution.py:506
  84.9 4.2 %collective-permute-start.11 = (bf16[128,256]{1,0:T(8,128)(2,1)S(1)}, bf16[128,256]{1,0:T(8,128)(2,1)S(1)}, u32[]{:S(2)}, u32[]{:S(2)}) collective-permute-start(bf16[128,256]{1,0:T(8,128)(2,1)S(1)} %get-tuple-element.122.grad0), channel_id=1, source_target_pairs={{0,3},{1,0},{2,1},{3,2},{4,7},{5,4},{6,5},{7,6},{8,11},{9,8},{10,9... | collective-permute-start | bytes 196616 | tf_op jit(solution)/shard_map/ppermute | solution.py:506
  86.2 4.3 %collective-permute-start.12 = (bf16[128,256]{1,0:T(8,128)(2,1)S(1)}, bf16[128,256]{1,0:T(8,128)(2,1)S(1)}, u32[]{:S(2)}, u32[]{:S(2)}) collective-permute-start(bf16[128,256]{1,0:T(8,128)(2,1)S(1)} %get-tuple-element.122.grad0), channel_id=1, source_target_pairs={{0,1},{1,2},{2,3},{3,0},{4,5},{5,6},{6,7},{7,4},{8,9},{9,10},{10,1... | collective-permute-start | bytes 196616 | tf_op jit(solution)/shard_map/ppermute | solution.py:506
  91.8 13.8 %collective-permute-start.16 = (bf16[16,192,128]{2,1,0:T(8,128)(2,1)S(1)}, bf16[16,192,128]{2,1,0:T(8,128)(2,1)S(1)}, u32[]{:S(2)}, u32[]{:S(2)}) collective-permute-start(bf16[16,192,128]{2,1,0:T(8,128)(2,1)S(1)} %get-tuple-element.80), channel_id=1, source_target_pairs={{0,4},{4,0},{8,12},{12,8},{16,20},{20,16},{24,28},{28,24},{32,36},... | collective-permute-start | bytes 2359304 | tf_op jit(solution)/shard_map/ppermute | solution.py:489
  97.0 6.4 %collective-permute-start.13 = (bf16[3,256,128]{2,1,0:T(8,128)(2,1)S(1)}, bf16[3,256,128]{2,1,0:T(8,128)(2,1)S(1)}, u32[]{:S(2)}, u32[]{:S(2)}) collective-permute-start(bf16[3,256,128]{2,1,0:T(8,128)(2,1)S(1)} %form_messages.1), channel_id=1, source_target_pairs={{0,64},{4,20},{8,72},{12,28},{16,80},{20,4},{24,88},{28,12},{32,96... | collective-permute-start | bytes 589832 | tf_op jit(solution)/shard_map/ppermute | solution.py:485
  98.4 7.1 %collective-permute-start.14 = (bf16[3,256,128]{2,1,0:T(8,128)(2,1)S(1)}, bf16[3,256,128]{2,1,0:T(8,128)(2,1)S(1)}, u32[]{:S(2)}, u32[]{:S(2)}) collective-permute-start(bf16[3,256,128]{2,1,0:T(8,128)(2,1)S(1)} %form_messages.1), channel_id=1, source_target_pairs={{0,32},{4,12},{8,40},{12,20},{16,48},{20,28},{24,56},{28,4},{32,64... | collective-permute-start | bytes 589832 | tf_op jit(solution)/shard_map/ppermute | solution.py:485
  99.8 5.7 %collective-permute-start.15 = (bf16[3,256,128]{2,1,0:T(8,128)(2,1)S(1)}, bf16[3,256,128]{2,1,0:T(8,128)(2,1)S(1)}, u32[]{:S(2)}, u32[]{:S(2)}) collective-permute-start(bf16[3,256,128]{2,1,0:T(8,128)(2,1)S(1)} %form_messages.1), channel_id=1, source_target_pairs={{0,96},{4,28},{8,104},{12,4},{16,112},{20,12},{24,120},{28,20},{32... | collective-permute-start | bytes 589832 | tf_op jit(solution)/shard_map/ppermute | solution.py:485
  105.6 29.6 %copy-start.7 = (bf16[12,256,128]{2,1,0:T(8,128)(2,1)}, bf16[12,256,128]{2,1,0:T(8,128)(2,1)S(1)}, u32[]{:S(2)}) copy-start(bf16[12,256,128]{2,1,0:T(8,128)(2,1)S(1)} %pad_maximum_fusion.own0) | copy-start | bytes 2359300
  105.8 8.3 %collective-permute-start.21 = (bf16[4,192,128]{2,1,0:T(8,128)(2,1)S(1)}, bf16[4,192,128]{2,1,0:T(8,128)(2,1)S(1)}, u32[]{:S(2)}, u32[]{:S(2)}) collective-permute-start(bf16[4,192,128]{2,1,0:T(8,128)(2,1)S(1)} %get-tuple-element.116), channel_id=1, source_target_pairs={{0,16},{4,68},{8,24},{12,76},{16,0},{20,84},{24,8},{28,92},{32,48}... | collective-permute-start | bytes 589832 | tf_op jit(solution)/shard_map/ppermute | solution.py:485
  107.4 27.7 %collective-permute-start.17 = (bf16[12,256,128]{2,1,0:T(8,128)(2,1)S(1)}, bf16[12,256,128]{2,1,0:T(8,128)(2,1)}, u32[]{:S(2)}, u32[]{:S(2)}) collective-permute-start(bf16[12,256,128]{2,1,0:T(8,128)(2,1)S(1)} %pad_maximum_fusion.own0), channel_id=1, source_target_pairs={{0,16},{4,68},{8,24},{12,76},{16,0},{20,84},{24,8},{28,92},{32,48}... | collective-permute-start | bytes 2359304 | tf_op jit(solution)/shard_map/ppermute | solution.py:485
  108.9 26.3 %collective-permute-start.18 = (bf16[12,256,128]{2,1,0:T(8,128)(2,1)S(1)}, bf16[12,256,128]{2,1,0:T(8,128)(2,1)}, u32[]{:S(2)}, u32[]{:S(2)}) collective-permute-start(bf16[12,256,128]{2,1,0:T(8,128)(2,1)S(1)} %pad_maximum_fusion.own0), channel_id=1, source_target_pairs={{0,8},{4,36},{8,16},{12,44},{16,24},{20,52},{24,0},{28,60},{32,40}... | collective-permute-start | bytes 2359304 | tf_op jit(solution)/shard_map/ppermute | solution.py:485
  109.2 26.0 %collective-permute-start.19 = (bf16[12,256,128]{2,1,0:T(8,128)(2,1)S(1)}, bf16[12,256,128]{2,1,0:T(8,128)(2,1)}, u32[]{:S(2)}, u32[]{:S(2)}) collective-permute-start(bf16[12,256,128]{2,1,0:T(8,128)(2,1)S(1)} %pad_maximum_fusion.own0), channel_id=1, source_target_pairs={{0,24},{4,100},{8,0},{12,108},{16,8},{20,116},{24,16},{28,124},{32... | collective-permute-start | bytes 2359304 | tf_op jit(solution)/shard_map/ppermute | solution.py:485
  110.3 24.8 %collective-permute-start.20 = (bf16[12,256,128]{2,1,0:T(8,128)(2,1)S(1)}, bf16[12,256,128]{2,1,0:T(8,128)(2,1)S(1)}, u32[]{:S(2)}, u32[]{:S(2)}) collective-permute-start(bf16[12,256,128]{2,1,0:T(8,128)(2,1)S(1)} %pad_maximum_fusion.own0), channel_id=1, source_target_pairs={{0,4},{4,0},{8,12},{12,8},{16,20},{20,16},{24,28},{28,24},{32,36},... | collective-permute-start | bytes 2359304 | tf_op jit(solution)/shard_map/ppermute | solution.py:489
  114.2 15.1 %collective-permute-start.22 = (bf16[4,192,128]{2,1,0:T(8,128)(2,1)S(1)}, bf16[4,192,128]{2,1,0:T(8,128)(2,1)S(1)}, u32[]{:S(2)}, u32[]{:S(2)}) collective-permute-start(bf16[4,192,128]{2,1,0:T(8,128)(2,1)S(1)} %get-tuple-element.115), channel_id=1, source_target_pairs={{0,8},{4,36},{8,16},{12,44},{16,24},{20,52},{24,0},{28,60},{32,40}... | collective-permute-start | bytes 589832 | tf_op jit(solution)/shard_map/ppermute | solution.py:485
  129.3 5.7 %collective-permute-start.23 = (bf16[4,192,128]{2,1,0:T(8,128)(2,1)S(1)}, bf16[4,192,128]{2,1,0:T(8,128)(2,1)S(1)}, u32[]{:S(2)}, u32[]{:S(2)}) collective-permute-start(bf16[4,192,128]{2,1,0:T(8,128)(2,1)S(1)} %get-tuple-element.114), channel_id=1, source_target_pairs={{0,24},{4,100},{8,0},{12,108},{16,8},{20,116},{24,16},{28,124},{32... | collective-permute-start | bytes 589832 | tf_op jit(solution)/shard_map/ppermute | solution.py:485
  135.2 15.8 %copy-start.10 = (bf16[12,256,128]{2,1,0:T(8,128)(2,1)}, bf16[12,256,128]{2,1,0:T(8,128)(2,1)S(1)}, u32[]{:S(2)}) copy-start(bf16[12,256,128]{2,1,0:T(8,128)(2,1)S(1)} %collective-permute-done.20.sib0) | copy-start | bytes 2359300
  135.2 16.6 %copy-start.3 = (bf16[96,128,128]{2,1,0:T(8,128)(2,1)S(1)}, bf16[96,128,128]{2,1,0:T(8,128)(2,1)}, u32[]{:S(2)}) copy-start(bf16[96,128,128]{2,1,0:T(8,128)(2,1)} %tiles1.3) | copy-start | bytes 9437188
  135.2 16.6 %collective-permute-start.27 = (bf16[12,256,128]{2,1,0:T(8,128)(2,1)}, bf16[12,256,128]{2,1,0:T(8,128)(2,1)}, u32[]{:S(2)}, u32[]{:S(2)}) collective-permute-start(bf16[12,256,128]{2,1,0:T(8,128)(2,1)} %collective-permute-done.17.own2), channel_id=1, source_target_pairs={{0,4},{4,0},{8,12},{12,8},{16,20},{20,16},{24,28},{28,24},{32,36},... | collective-permute-start | bytes 2359304 | tf_op jit(solution)/shard_map/ppermute | solution.py:489
  139.5 12.4 %collective-permute-start.28 = (bf16[12,256,128]{2,1,0:T(8,128)(2,1)}, bf16[12,256,128]{2,1,0:T(8,128)(2,1)}, u32[]{:S(2)}, u32[]{:S(2)}) collective-permute-start(bf16[12,256,128]{2,1,0:T(8,128)(2,1)} %collective-permute-done.18.own3), channel_id=1, source_target_pairs={{0,4},{4,0},{8,12},{12,8},{16,20},{20,16},{24,28},{28,24},{32,36},... | collective-permute-start | bytes 2359304 | tf_op jit(solution)/shard_map/ppermute | solution.py:489
  139.6 12.3 %collective-permute-start.29 = (bf16[12,256,128]{2,1,0:T(8,128)(2,1)}, bf16[12,256,128]{2,1,0:T(8,128)(2,1)}, u32[]{:S(2)}, u32[]{:S(2)}) collective-permute-start(bf16[12,256,128]{2,1,0:T(8,128)(2,1)} %collective-permute-done.19.own1), channel_id=1, source_target_pairs={{0,4},{4,0},{8,12},{12,8},{16,20},{20,16},{24,28},{28,24},{32,36},... | collective-permute-start | bytes 2359304 | tf_op jit(solution)/shard_map/ppermute | solution.py:489
  140.0 4.4 %collective-permute-start.24 = (bf16[192,128]{1,0:T(8,128)(2,1)S(1)}, bf16[192,128]{1,0:T(8,128)(2,1)S(1)}, u32[]{:S(2)}, u32[]{:S(2)}) collective-permute-start(bf16[192,128]{1,0:T(8,128)(2,1)S(1)} %get-tuple-element.88), channel_id=1, source_target_pairs={{0,64},{4,20},{8,72},{12,28},{16,80},{20,4},{24,88},{28,12},{32,96... | collective-permute-start | bytes 147464 | tf_op jit(solution)/shard_map/ppermute | solution.py:485
  141.3 9.7 %collective-permute-start.25 = (bf16[192,128]{1,0:T(8,128)(2,1)S(1)}, bf16[192,128]{1,0:T(8,128)(2,1)S(1)}, u32[]{:S(2)}, u32[]{:S(2)}) collective-permute-start(bf16[192,128]{1,0:T(8,128)(2,1)S(1)} %get-tuple-element.89), channel_id=1, source_target_pairs={{0,32},{4,12},{8,40},{12,20},{16,48},{20,28},{24,56},{28,4},{32,64... | collective-permute-start | bytes 147464 | tf_op jit(solution)/shard_map/ppermute | solution.py:485
  144.4 6.6 %collective-permute-start.26 = (bf16[192,128]{1,0:T(8,128)(2,1)S(1)}, bf16[192,128]{1,0:T(8,128)(2,1)S(1)}, u32[]{:S(2)}, u32[]{:S(2)}) collective-permute-start(bf16[192,128]{1,0:T(8,128)(2,1)S(1)} %get-tuple-element.90), channel_id=1, source_target_pairs={{0,96},{4,28},{8,104},{12,4},{16,112},{20,12},{24,120},{28,20},{32... | collective-permute-start | bytes 147464 | tf_op jit(solution)/shard_map/ppermute | solution.py:485
  151.9 2.8 %copy-start.1 = (bf16[192,128,128]{2,1,0:T(8,128)(2,1)S(1)}, bf16[192,128,128]{2,1,0:T(8,128)(2,1)}, u32[]{:S(2)}) copy-start(bf16[192,128,128]{2,1,0:T(8,128)(2,1)} %tiles0.3) | copy-start | bytes 18874372
  154.7 1.4 copy-start.6
  156.1 1.1 copy-start.8
  157.2 1.1 copy-start.11
  (3 other events, 2.0 us)
